TPU v7x, 512 devices: a whole 4x8x8 slice. The times are simulated.
512 devices in a mesh: head: 32 (over x, y), kv: 16 (over z, core).
Axes of the slice: x: 4, y: 8, z: 8, core: 2. Of those that a mesh axis runs over, the one named last changes fastest.
Arguments:
- queries: bfloat16 [2048, 4096], P(('head', 'kv')), may hold values from -240 to 240
- new_keys: bfloat16 [2048, 1024], P(('head', 'kv')), may hold values from -6 to 6
- new_values: bfloat16 [2048, 1024], P(('head', 'kv')), may hold values from -6 to 6
- cache_keys: bfloat16 [8, 16384, 128], P(None, 'kv'), may hold values from -6 to 6
- cache_values: bfloat16 [8, 16384, 128], P(None, 'kv'), may hold values from -6 to 6
- start: int32 [1], replicated, may hold values from 16384 to 28672
Outputs:
- attended: bfloat16 [2048, 4096], P(('head', 'kv'))
All inputs are finite; a program needn't handle non-finite values.
Results may differ from a plain program's by a relative error of at most 0.034.
Values may be sent and summed in bfloat16 or wider, within the bound.
A program may use at most 128 MiB of HBM per device.

v0:
```python
import jax
import jax.numpy as jnp
from jax import lax
from jax.sharding import PartitionSpec as P

HEADS = 32
KVH = 8
HD = 128


THETA = 500000.0


def combined_all(value, axis, join):
    pieces = jax.tree.map(lambda part: lax.all_gather(part, axis), value)
    head = jax.tree.map(lambda part: part[0], pieces)
    tail = jax.tree.map(lambda part: part[1:], pieces)
    total, _ = lax.scan(lambda total, piece: (join(total, piece), None), head, tail)
    return total


def frequencies(width):
    half = width // 2
    base = jnp.power(THETA, -(jnp.arange(half, dtype=jnp.float32) * 2.0 / width))
    wave = 2.0 * jnp.pi / base
    smooth = (8192.0 / wave - 1.0) / 3.0
    blended = (1.0 - smooth) * base / 8.0 + smooth * base
    return jnp.where(wave < 2048.0, base, jnp.where(wave > 8192.0, base / 8.0, blended))


def rotate(field, places):
    half = field.shape[-1] // 2
    freq = frequencies(field.shape[-1])
    angle = places.astype(jnp.float32)[:, None] * freq[None, :]
    cosine = jnp.cos(angle)[:, None, :]
    sine = jnp.sin(angle)[:, None, :]
    values = field.astype(jnp.float32)
    first = values[..., :half]
    second = values[..., half:]
    return jnp.concatenate(
        [first * cosine - second * sine, second * cosine + first * sine], -1
    ).astype(jnp.bfloat16)


def partials(query_head, query_places, cached_k, cached_v, fresh_k, fresh_v, key_places):
    count = query_head.shape[0]
    block = min(512, count)
    nblocks = count // block
    scale = HD ** (-0.5)

    def one_block(index):
        first = index * block
        query_rows = lax.dynamic_slice_in_dim(query_head, first, block, 0)
        targets = lax.dynamic_slice_in_dim(query_places, first, block, 0)
        scores_old = jnp.dot(query_rows, cached_k.T, preferred_element_type=jnp.float32) * scale
        scores_new = jnp.dot(query_rows, fresh_k.T, preferred_element_type=jnp.float32) * scale
        visible = key_places[None, :] <= targets[:, None]
        scores_new = jnp.where(visible, scores_new, -1e30)
        top = jnp.maximum(jnp.max(scores_old, 1), jnp.max(scores_new, 1))
        probs_old = jnp.exp(scores_old - top[:, None]).astype(jnp.bfloat16)
        probs_new = jnp.where(visible, jnp.exp(scores_new - top[:, None]), 0.0).astype(jnp.bfloat16)
        total = jnp.sum(probs_old.astype(jnp.float32), 1) + jnp.sum(
            probs_new.astype(jnp.float32), 1
        )
        output = jnp.dot(probs_old, cached_v, preferred_element_type=jnp.float32)
        output = output + jnp.dot(probs_new, fresh_v, preferred_element_type=jnp.float32)
        return (top, total, output)

    top, total, output = lax.map(one_block, jnp.arange(nblocks, dtype=jnp.int32))
    return (top.reshape(count), total.reshape(count), output.reshape(count, HD))


def combine(left, right):
    top = jnp.maximum(left[0], right[0])
    scale_left = jnp.exp(left[0] - top)
    scale_right = jnp.exp(right[0] - top)
    total = left[1] * scale_left + right[1] * scale_right
    output = left[2] * scale_left[..., None] + right[2] * scale_right[..., None]
    return (top, total, output)


def shards(queries, new_keys, new_values, cache_keys, cache_values, start):
    head_count = lax.axis_size("head")
    kv_count = lax.axis_size("kv")
    head_index = lax.axis_index("head")
    kv_index = lax.axis_index("kv")
    tok_rows = queries.shape[0]
    per_device = HEADS // head_count
    group = HEADS // KVH
    block_index = head_index * kv_count + kv_index
    places = start[0] + block_index * tok_rows + jnp.arange(tok_rows, dtype=jnp.int32)
    rotated = rotate(queries.reshape(tok_rows, HEADS, HD), places).reshape(tok_rows, HEADS * HD)
    keys_rot = rotate(new_keys.reshape(tok_rows, KVH, HD), places)
    keys_wide = jnp.repeat(keys_rot, group, axis=1).reshape(tok_rows, HEADS * HD)
    values_wide = jnp.repeat(new_values.reshape(tok_rows, KVH, HD), group, axis=1).reshape(
        tok_rows, HEADS * HD
    )
    mine_q, mine_k, mine_v = (
        lax.all_to_all(rotated, "head", split_axis=1, concat_axis=0, tiled=True),
        lax.all_to_all(keys_wide, "head", split_axis=1, concat_axis=0, tiled=True),
        lax.all_to_all(values_wide, "head", split_axis=1, concat_axis=0, tiled=True),
    )
    span = tok_rows * head_count
    within = jnp.arange(span, dtype=jnp.int32)
    key_places = (within // tok_rows * kv_count + kv_index) * tok_rows + within % tok_rows
    gathered = lax.all_gather(mine_q, "kv", axis=0, tiled=True)
    overall = span * kv_count
    global_rows = jnp.arange(overall, dtype=jnp.int32)
    source = global_rows // span
    inside = global_rows % span
    query_places = (inside // tok_rows * kv_count + source) * tok_rows + inside % tok_rows
    kv_head = head_index * per_device // group
    cached_k = lax.dynamic_index_in_dim(cache_keys, kv_head, 0, keepdims=False)
    cached_v = lax.dynamic_index_in_dim(cache_values, kv_head, 0, keepdims=False)
    tops, totals, outputs = ([], [], [])
    top, total, output = partials(
        gathered, query_places, cached_k, cached_v, mine_k, mine_v, key_places
    )
    tops.append(top)
    totals.append(total)
    outputs.append(output)
    top = jnp.stack(tops)
    total = jnp.stack(totals)
    output = jnp.stack(outputs)
    top, total, output = combined_all((top, total, output), "kv", combine)
    total = lax.dynamic_slice_in_dim(total, kv_index * span, span, 1)
    output = lax.dynamic_slice_in_dim(output, kv_index * span, span, 1)
    result = (output / total[..., None]).astype(jnp.bfloat16)
    result = jnp.transpose(result, (1, 0, 2)).reshape(span, per_device * HD)
    return lax.all_to_all(result, "head", split_axis=0, concat_axis=1, tiled=True)


def solution(mesh):
    placed = (
        P(("head", "kv"), None),
        P(("head", "kv"), None),
        P(("head", "kv"), None),
        P(None, "kv", None),
        P(None, "kv", None),
        P(),
    )
    return jax.shard_map(
        shards, mesh=mesh, in_specs=placed, out_specs=P(("head", "kv"), None), check_vma=False
    )
```

profile of v0, /device:TPU:1, one launch (start us, length us, event | category | flops | bytes accessed | tf_op | source)
XLA Modules:
  0.0 259.6 jit_solution(10179479059133996901)
XLA Ops:
  8.9 10.5 %all-to-all-start = ((bf16[4,32,128]{2,0,1:T(4,128)(2,1)}), bf16[4,32,128]{2,0,1:T(4,128)(2,1)S(1)}, u32[]{:S(2)}, u32[]{:S(2)}) async-start(bf16[4,32,128]{2,0,1:T(4,128)(2,1)} %pad_maximum_fusion), calls=%async_computation | async-start | bytes 65536 | tf_op jit(solution)/shard_map/all_to_all | solution.py:99
  20.4 1.1 dynamic-slice_bitcast_fusion
  21.4 6.8 %all-to-all-done = bf16[4,32,128]{2,0,1:T(4,128)(2,1)S(1)} async-done(((bf16[4,32,128]{2,0,1:T(4,128)(2,1)}), bf16[4,32,128]{2,0,1:T(4,128)(2,1)S(1)}, u32[]{:S(2)}, u32[]{:S(2)}) %all-to-all-start) | async-done | bytes 32800 | tf_op jit(solution)/shard_map/all_to_all | solution.py:99
  28.8 3.9 %all-to-all-start.1 = ((bf16[4,32,128]{2,0,1:T(4,128)(2,1)}), bf16[4,32,128]{2,0,1:T(4,128)(2,1)S(1)}, u32[]{:S(2)}, u32[]{:S(2)}) async-start(bf16[4,32,128]{2,0,1:T(4,128)(2,1)} %bitcast.11), calls=%async_computation.1 | async-start | bytes 65536 | tf_op jit(solution)/shard_map/all_to_all | solution.py:100
  32.7 8.7 %all-to-all-done.1 = bf16[4,32,128]{2,0,1:T(4,128)(2,1)S(1)} async-done(((bf16[4,32,128]{2,0,1:T(4,128)(2,1)}), bf16[4,32,128]{2,0,1:T(4,128)(2,1)S(1)}, u32[]{:S(2)}, u32[]{:S(2)}) %all-to-all-start.1) | async-done | bytes 32800 | tf_op jit(solution)/shard_map/all_to_all | solution.py:100
  41.4 1.3 broadcast_in_dim.26
  42.7 3.9 %all-to-all-start.2 = ((bf16[4,32,128]{2,0,1:T(4,128)(2,1)}), bf16[4,32,128]{2,0,1:T(4,128)(2,1)S(1)}, u32[]{:S(2)}, u32[]{:S(2)}) async-start(bf16[4,32,128]{2,0,1:T(4,128)(2,1)} %bitcast.16), calls=%async_computation.2 | async-start | bytes 65536 | tf_op jit(solution)/shard_map/all_to_all | solution.py:101
  46.6 27.7 %all_gather.12 = bf16[2048,128]{1,0:T(8,128)(2,1)S(1)} all-gather(bf16[128,128]{1,0:T(8,128)(2,1)S(1)} %bitcast.102), channel_id=1, replica_groups=mesh['head'=32,'kv'=16] {'kv'}, dimensions={0}, use_global_device_ids=true | all-gather | bytes 557056 | tf_op jit(solution)/shard_map/all_gather | solution.py:106
  74.3 17.2 %while.30 = (s32[]{:T(128)}, f32[4,512]{1,0:T(4,128)S(1)}, f32[4,512]{1,0:T(4,128)S(1)}, f32[4,512,128]{2,1,0:T(8,128)}, s32[4]{0:T(128)S(1)}, /*index=5*/bf16[2...) while((s32[]{:T(128)}, f32[4,512]{1,0:T(4,128)S(1)}, ...), condition=%wide.region_5.6_spmd.clone, body=%wide.region_0.5_spmd.clone.sunk | while | flops 306643968 | bytes 8764135 | solution.py:69
  81.7 1.0 fusion.69
  91.6 14.8 %all_gather.13 = f32[16,1,2048]{2,1,0:T(1,128)S(1)} all-gather(f32[1,1,2048]{2,1,0:T(1,128)S(1)} %all_gather_stack_reshape.9), channel_id=1, replica_groups=mesh['head'=32,'kv'=16] {'kv'}, dimensions={0}, use_global_device_ids=true | all-gather | bytes 139264 | tf_op jit(solution)/shard_map/all_gather | solution.py:15
  106.4 16.7 %all_gather.14 = f32[16,1,2048]{2,1,0:T(1,128)S(1)} all-gather(f32[1,1,2048]{2,1,0:T(1,128)S(1)} %all_gather_stack_reshape.10), channel_id=1, replica_groups=mesh['head'=32,'kv'=16] {'kv'}, dimensions={0}, use_global_device_ids=true | all-gather | bytes 139264 | tf_op jit(solution)/shard_map/all_gather | solution.py:15
  123.2 64.9 %all-gather.2.cloned.1.call-done = f32[16,1,2048,128]{3,2,1,0:T(8,128)} async-done(((f32[1,1,2048,128]{3,2,1,0:T(8,128)}), f32[16,1,2048,128]{3,2,1,0:T(8,128)}) %all-gather.2.cloned.1.call-update) | async-done | bytes 16777232 | tf_op jit(solution)/shard_map/all_gather | solution.py:15
  188.1 12.4 %slice.49 = f32[15,1,2048,128]{3,2,1,0:T(8,128)} slice(f32[16,1,2048,128]{3,2,1,0:T(8,128)} %all-gather.2.cloned.1.call-done), slice={[1:16], [0:1], [0:2048], [0:128]} | slice | bytes 31457280 | tf_op jit(solution)/shard_map/slice | solution.py:17
  200.5 1.3 slice_bitcast_fusion
  201.8 32.3 %while.29 = (s32[]{:T(128)}, f32[1,2048]{1,0:T(1,128)S(1)}, f32[1,2048]{1,0:T(1,128)S(1)}, f32[1,2048,128]{2,1,0:T(8,128)S(1)}, f32[15,1,2048]{2,1,0:T(1,128)S(1...) while((s32[]{:T(128)}, f32[1,2048]{1,0:T(1,128)S(1)}, ...), condition=%wide.region_7.8_spmd, body=%wide.region_6.7_spmd.sunk | while | flops 798722 | bytes 3227741 | solution.py:18
  201.9 2.1 fusion.59
  204.0 2.1 fusion.59
  206.2 2.1 fusion.59
  208.3 2.1 fusion.59
  210.5 2.1 fusion.59
  212.6 2.1 fusion.59
  214.8 2.1 fusion.59
  216.9 2.1 fusion.59
  219.1 2.1 fusion.59
  221.3 2.1 fusion.59
  223.4 2.1 fusion.59
  225.6 2.1 fusion.59
  227.7 2.1 fusion.59
  229.9 2.1 fusion.59
  232.0 2.1 fusion.59
  234.3 17.9 %all_to_all.73 = bf16[32,4,128]{2,1,0:T(4,128)(2,1)S(1)} all-to-all(bf16[32,4,128]{2,1,0:T(4,128)(2,1)S(1)} %bitcast.103), channel_id=1, replica_groups=mesh['head'=32,'kv'=16] {'head'}, dimensions={0} | all-to-all | bytes 65536 | tf_op jit(solution)/shard_map/all_to_all | solution.py:130
  (95 shorter events, 18.3 us)
Async XLA Ops:
  8.9 19.3 %all-to-all-start = ((bf16[4,32,128]{2,0,1:T(4,128)(2,1)}), bf16[4,32,128]{2,0,1:T(4,128)(2,1)S(1)}, u32[]{:S(2)}, u32[]{:S(2)}) async-start(bf16[4,32,128]{2,0,1:T(4,128)(2,1)} %pad_maximum_fusion), calls=%async_computation | async-start | bytes 65536 | tf_op jit(solution)/shard_map/all_to_all | solution.py:99
  28.8 12.6 %all-to-all-start.1 = ((bf16[4,32,128]{2,0,1:T(4,128)(2,1)}), bf16[4,32,128]{2,0,1:T(4,128)(2,1)S(1)}, u32[]{:S(2)}, u32[]{:S(2)}) async-start(bf16[4,32,128]{2,0,1:T(4,128)(2,1)} %bitcast.11), calls=%async_computation.1 | async-start | bytes 65536 | tf_op jit(solution)/shard_map/all_to_all | solution.py:100
  42.7 31.6 %all-to-all-start.2 = ((bf16[4,32,128]{2,0,1:T(4,128)(2,1)}), bf16[4,32,128]{2,0,1:T(4,128)(2,1)S(1)}, u32[]{:S(2)}, u32[]{:S(2)}) async-start(bf16[4,32,128]{2,0,1:T(4,128)(2,1)} %bitcast.16), calls=%async_computation.2 | async-start | bytes 65536 | tf_op jit(solution)/shard_map/all_to_all | solution.py:101
  46.6 141.5 %all-gather.2.cloned.1.call-start = ((), (), s32[]{:S(2)}) async-start(), calls=%async_computation.4 | async-start | bytes 17825792 | tf_op jit(solution)/shard_map/all_gather | solution.py:15
Sparse Core Ops, SparseCore 0:
  91.7 96.3 all-gather.1
where the time goes:
time: 261 us; the launch traced here: 260 us
  waiting for transfers between devices  80.4 us (31%)
  blocking collectives  77.1 us (30%)
  other arithmetic  37.5 us (14%)
  local copies, waits for them, and re-layouts  20.5 us (8%)
  starting transfers between devices  18.2 us (7%)
  between operations  14.2 us (5%)
  matrix products  8.65 us (3%)
  loops' own time  3.05 us (1%)
    all_gather x1, waiting for transfers between devices, combined_all(): pieces = jax.tree.map(lambda part: lax.all_gather(part, axis), value)  64.9 us
    all_gather x2, blocking collectives, combined_all(): pieces = jax.tree.map(lambda part: lax.all_gather(part, axis), value)  31.5 us
    add x15, other arithmetic, combine(): output = left[2] * scale_left[..., None] + right[2] * scale_right[..., None]  31.3 us
    all_gather x1, blocking collectives, shards(): gathered = lax.all_gather(mine_q, 'kv', axis=0, tiled=True)  27.7 us
    all_to_all x1, blocking collectives, shards(): lax.all_to_all(result, 'head', split_axis=0, concat_axis=1, tiled=True)  17.9 us
    slice x3, local copies, waits for them, and re-layouts, combined_all(): tail = jax.tree.map(lambda part: part[1:], pieces)  12.4 us
    all_to_all x1, starting transfers between devices, shards(): lax.all_to_all(rotated, 'head', split_axis=1, concat_axis=0, tiled=True)  10.5 us
    all_to_all x1, waiting for transfers between devices, shards(): lax.all_to_all(keys_wide, 'head', split_axis=1, concat_axis=0, tiled=True)  8.68 us
  transfers between devices with their start and end apart: 4, of which 3 were waited for; matrix products, arithmetic and copies ran while one was open for 1% of the time, Pallas kernels for 0%

commit v1 on v0

v1 whole, which is shorter than its diff:
```python
import functools
import math

import jax
import jax.numpy as jnp
import numpy as np
from jax import lax
from jax.experimental import pallas as pl
from jax.experimental.pallas import tpu as pltpu
from jax.sharding import PartitionSpec as P

HEADS = 32
KVH = 8
HD = 128
GROUP = HEADS // KVH
THETA = 500000.0
MESH = pl.DeviceIdType.MESH

NX, NY, NZ, NC = 4, 8, 8, 2
NG = NX * NC
TOK = 4
ROWS = TOK * GROUP
CHUNK = NG * ROWS
EXP_SCALE = HD ** (-0.5) * math.log2(math.e)


def frequencies():
    half = HD // 2
    base = THETA ** (-(np.arange(half, dtype=np.float64) * 2.0 / HD))
    wave = 2.0 * np.pi / base
    smooth = (8192.0 / wave - 1.0) / 3.0
    blended = (1.0 - smooth) * base / 8.0 + smooth * base
    freq = np.where(wave < 2048.0, base, np.where(wave > 8192.0, base / 8.0, blended))
    return np.concatenate([freq, freq]).astype(np.float32)[None, :]


def kernel(
    start_ref, freq_ref, q_ref, k_ref, v_ref, ck_ref, cv_ref, o_ref,
    sq, skv, qall, kvall, kbuf, vbuf, so, ss, ro, rs, sf, of,
    csem, xsend, xrecv, qsend, qrecv, fsend, frecv, osend, orecv, ssend, srecv, rsend, rrecv,
):
    cached = ck_ref.shape[1]
    head, kv = lax.axis_index("head"), lax.axis_index("kv")
    x, y = lax.div(head, NY), lax.rem(head, NY)
    z, c = lax.div(kv, NC), lax.rem(kv, NC)
    g = x * NC + c

    def of_group(other):
        return (lax.div(other, NC) * NY + y, z * NC + lax.rem(other, NC))

    def of_plane(other):
        return (head, other * NC + c)

    def of_row(other):
        return (x * NY + other, kv)

    groups = [lax.rem(g + i, NG) for i in range(1, NG)]
    planes = [lax.rem(z + i, NZ) for i in (1, 7, 2, 6, 3, 5, 4)]
    rows = [lax.rem(y + i, NY) for i in (1, 7, 2, 6, 3, 5, 4)]

    own_k = pltpu.make_async_copy(ck_ref.at[g], kbuf.at[pl.ds(0, cached)], csem.at[0])
    own_v = pltpu.make_async_copy(cv_ref.at[g], vbuf.at[pl.ds(0, cached)], csem.at[1])
    own_k.start()
    own_v.start()

    barrier = pltpu.get_barrier_semaphore()
    peers = [of_group(i) for i in groups] + [of_plane(i) for i in planes] + [of_row(i) for i in rows]
    for peer in peers:
        pl.semaphore_signal(barrier, inc=1, device_id=peer, device_id_type=MESH)

    first = start_ref[0] + (head * (NZ * NC) + kv) * TOK
    places = first + lax.broadcasted_iota(jnp.int32, (TOK, HD), 0)
    angle = places.astype(jnp.float32) * freq_ref[...]
    lane = lax.broadcasted_iota(jnp.int32, (TOK, HD), 1)
    cosine = jnp.cos(angle)
    sine = jnp.sin(angle)
    sine = jnp.where(lane < HD // 2, -sine, sine)
    cos_q = jnp.concatenate([cosine] * GROUP, 0)
    sin_q = jnp.concatenate([sine] * GROUP, 0)
    for i in range(NG):
        part = jnp.concatenate(
            [
                q_ref[:, (i * GROUP + j) * HD : (i * GROUP + j + 1) * HD].astype(jnp.float32)
                for j in range(GROUP)
            ],
            0,
        )
        turned = part * cos_q + pltpu.roll(part, HD // 2, 1) * sin_q
        sq[i] = turned.astype(jnp.bfloat16)
        part = k_ref[:, i * HD : (i + 1) * HD].astype(jnp.float32)
        turned = part * cosine + pltpu.roll(part, HD // 2, 1) * sine
        value = v_ref[:, i * HD : (i + 1) * HD].astype(jnp.float32)
        skv[i] = jnp.concatenate([turned, value], 0).astype(jnp.bfloat16)

    pl.semaphore_wait(barrier, len(peers))

    sends = []
    partner = x * NC + (1 - c)
    for i in groups:
        copy = pltpu.make_async_remote_copy(
            src_ref=sq.at[i], dst_ref=qall.at[z, g], send_sem=xsend.at[0, i],
            recv_sem=xrecv.at[0, g], device_id=of_group(i), device_id_type=MESH,
        )
        copy.start()
        sends.append(copy)
        copy = pltpu.make_async_remote_copy(
            src_ref=skv.at[i], dst_ref=kvall.at[y, g], send_sem=xsend.at[1, i],
            recv_sem=xrecv.at[1, g], device_id=of_group(i), device_id_type=MESH,
        )
        copy.start()
        sends.append(copy)
    for i, (source, target) in enumerate(((ck_ref, kbuf), (cv_ref, vbuf))):
        copy = pltpu.make_async_remote_copy(
            src_ref=source.at[partner], dst_ref=target.at[pl.ds(cached, cached)],
            send_sem=csem.at[2 + i], recv_sem=csem.at[4 + i],
            device_id=of_group(partner), device_id_type=MESH,
        )
        copy.start()
        sends.append(copy)
    qall[z, g] = sq[g]
    kvall[y, g] = skv[g]

    for i in groups:
        pltpu.make_async_copy(qall.at[z, i], qall.at[z, i], xrecv.at[0, i]).wait()
    for i in planes:
        copy = pltpu.make_async_remote_copy(
            src_ref=qall.at[z], dst_ref=qall.at[z], send_sem=qsend.at[i],
            recv_sem=qrecv.at[z], device_id=of_plane(i), device_id_type=MESH,
        )
        copy.start()
        sends.append(copy)
    for i in groups:
        pltpu.make_async_copy(kvall.at[y, i], kvall.at[y, i], xrecv.at[1, i]).wait()
    for i in rows:
        copy = pltpu.make_async_remote_copy(
            src_ref=kvall.at[y], dst_ref=kvall.at[y], send_sem=fsend.at[i],
            recv_sem=frecv.at[y], device_id=of_row(i), device_id_type=MESH,
        )
        copy.start()
        sends.append(copy)

    own_k.wait()
    own_v.wait()
    for i, target in enumerate((kbuf, vbuf)):
        half = target.at[pl.ds(cached, cached)]
        pltpu.make_async_copy(half, half, csem.at[4 + i]).wait()
    for i in rows:
        pltpu.make_async_copy(kvall.at[i], kvall.at[i], frecv.at[i]).wait()

    for i in range(NY):
        for j in range(NG // 4):
            four = [kvall[i, j * 4 + n].astype(jnp.float32) for n in range(4)]
            place = 2 * cached + (i * NG + j * 4) * TOK
            kbuf[place : place + 16] = jnp.concatenate(
                [one[:TOK] for one in four], 0
            ).astype(jnp.bfloat16)
            vbuf[place : place + 16] = jnp.concatenate(
                [one[TOK:] for one in four], 0
            ).astype(jnp.bfloat16)

    fresh = NY * NG * TOK
    wide = 2 * CHUNK
    row = lax.broadcasted_iota(jnp.int32, (wide, fresh), 0)
    column = lax.broadcasted_iota(jnp.int32, (wide, fresh), 1)
    row_group = lax.rem(lax.div(row, ROWS), NG)
    row_token = (lax.div(row_group, NC) * NY + y) * (NZ * NC * TOK) + (
        lax.rem(row_group, NC) * TOK + lax.rem(row, TOK)
    )
    column_group = lax.rem(lax.div(column, TOK), NG)
    column_token = (
        lax.div(column_group, NC) * NY + lax.div(column, NG * TOK)
    ) * (NZ * NC * TOK) + (lax.rem(column_group, NC) * TOK + lax.rem(column, TOK))
    behind = row_token - column_token - z * (NC * TOK)
    square = (CHUNK, CHUNK)
    diagonal = lax.broadcasted_iota(jnp.int32, square, 0) == lax.broadcasted_iota(
        jnp.int32, square, 1
    )
    ones = jnp.ones((2 * cached + fresh, HD), jnp.bfloat16)

    def chunk(i, carry):
        pair = (lax.rem(z - i + NZ, NZ), lax.rem(z + i + 1, NZ))

        @pl.when(i > 0)
        def _():
            pltpu.make_async_copy(qall.at[pair[0]], qall.at[pair[0]], qrecv.at[pair[0]]).wait()

        pltpu.make_async_copy(qall.at[pair[1]], qall.at[pair[1]], qrecv.at[pair[1]]).wait()
        queries = jnp.concatenate([qall[one].reshape(CHUNK, HD) for one in pair], 0)
        scores = lax.dot_general(
            queries, kbuf[...], (((1,), (1,)), ((), ())), preferred_element_type=jnp.float32
        )
        plane = jnp.where(row < CHUNK, pair[0], pair[1]) * (NC * TOK)
        old, new = scores[:, : 2 * cached], scores[:, 2 * cached :]
        new = jnp.where(behind + plane >= 0, new, -1e30)
        top = jnp.maximum(jnp.max(old, 1, keepdims=True), jnp.max(new, 1, keepdims=True))
        top = top * EXP_SCALE
        scores = jnp.concatenate([old, new], 1)
        probs = jnp.exp2(scores * EXP_SCALE - top).astype(jnp.bfloat16)
        both = jnp.dot(
            probs, jnp.concatenate([vbuf[...], ones], 1), preferred_element_type=jnp.float32
        )
        total = both[:, HD:]
        level = top + jnp.log2(total)
        output = (both[:, :HD] / total).astype(jnp.bfloat16)
        for n in range(2):
            part = slice(n * CHUNK, (n + 1) * CHUNK)
            flat = jnp.sum(jnp.where(diagonal, level[part], 0.0), 0, keepdims=True)
            so[pair[n]] = output[part]
            ss[pair[n]] = flat

        def give(other):
            for source, target, sent, got in ((so, ro, osend, orecv), (ss, rs, ssend, srecv)):
                pltpu.make_async_remote_copy(
                    src_ref=source.at[other], dst_ref=target.at[z], send_sem=sent.at[other],
                    recv_sem=got.at[z], device_id=of_plane(other), device_id_type=MESH,
                ).start()

        @pl.when(i > 0)
        def _():
            give(pair[0])

        give(pair[1])
        return carry

    lax.fori_loop(0, NZ // 2, chunk, 0)
    ro[z] = so[z]
    rs[z] = ss[z]

    for i in planes:
        pltpu.make_async_copy(rs.at[i], rs.at[i], srecv.at[i]).wait()
        pltpu.make_async_copy(ro.at[i], ro.at[i], orecv.at[i]).wait()
    levels = rs[:, 0, :]
    weight = jnp.exp2(levels - jnp.max(levels, 0, keepdims=True))
    weight = weight / jnp.sum(weight, 0, keepdims=True)
    weight = jnp.transpose(weight)
    total = weight[:, 0:1] * ro[0].astype(jnp.float32)
    for i in range(1, NZ):
        total = total + weight[:, i : i + 1] * ro[i].astype(jnp.float32)
    sf[...] = total.astype(jnp.bfloat16).reshape(NG, ROWS, HD)
    for i in groups:
        copy = pltpu.make_async_remote_copy(
            src_ref=sf.at[i], dst_ref=of.at[g], send_sem=rsend.at[i],
            recv_sem=rrecv.at[g], device_id=of_group(i), device_id_type=MESH,
        )
        copy.start()
        sends.append(copy)
    of[g] = sf[g]
    for i in groups:
        pltpu.make_async_copy(of.at[i], of.at[i], rrecv.at[i]).wait()
    for i in range(NG):
        part = of[i].astype(jnp.float32)
        for j in range(GROUP):
            o_ref[:, (i * GROUP + j) * HD : (i * GROUP + j + 1) * HD] = part[
                j * TOK : (j + 1) * TOK
            ].astype(jnp.bfloat16)

    for copy in sends:
        copy.wait_send()
    for i in planes:
        for source, sent in ((so, osend), (ss, ssend)):
            pltpu.make_async_copy(source.at[i], source.at[i], sent.at[i]).wait()


def shards(queries, new_keys, new_values, cache_keys, cache_values, start):
    cached = cache_keys.shape[1]
    keys = 2 * cached + NY * NG * TOK
    vmem = pl.BlockSpec(memory_space=pltpu.VMEM)
    hbm = pl.BlockSpec(memory_space=pl.ANY)
    dma = pltpu.SemaphoreType.DMA
    bf16 = jnp.bfloat16
    return pl.pallas_call(
        kernel,
        out_shape=jax.ShapeDtypeStruct((TOK, HEADS * HD), bf16),
        in_specs=[pl.BlockSpec(memory_space=pltpu.SMEM), vmem, vmem, vmem, vmem, hbm, hbm],
        out_specs=vmem,
        scratch_shapes=[
            pltpu.VMEM((NG, ROWS, HD), bf16),
            pltpu.VMEM((NG, 2 * TOK, HD), bf16),
            pltpu.VMEM((NZ, NG, ROWS, HD), bf16),
            pltpu.VMEM((NY, NG, 2 * TOK, HD), bf16),
            pltpu.VMEM((keys, HD), bf16),
            pltpu.VMEM((keys, HD), bf16),
            pltpu.VMEM((NZ, CHUNK, HD), bf16),
            pltpu.VMEM((NZ, 1, CHUNK), jnp.float32),
            pltpu.VMEM((NZ, CHUNK, HD), bf16),
            pltpu.VMEM((NZ, 1, CHUNK), jnp.float32),
            pltpu.VMEM((NG, ROWS, HD), bf16),
            pltpu.VMEM((NG, ROWS, HD), bf16),
            dma((6,)), dma((2, NG)), dma((2, NG)), dma((NZ,)), dma((NZ,)), dma((NY,)), dma((NY,)),
            dma((NZ,)), dma((NZ,)), dma((NZ,)), dma((NZ,)), dma((NG,)), dma((NG,)),
        ],
        compiler_params=pltpu.CompilerParams(
            collective_id=0, has_side_effects=True, vmem_limit_bytes=60000 * 1024
        ),
    )(start, jnp.asarray(frequencies()), queries, new_keys, new_values, cache_keys, cache_values)


def solution(mesh):
    placed = (
        P(("head", "kv"), None),
        P(("head", "kv"), None),
        P(("head", "kv"), None),
        P(None, "kv", None),
        P(None, "kv", None),
        P(),
    )
    return jax.shard_map(
        shards, mesh=mesh, in_specs=placed, out_specs=P(("head", "kv"), None), check_vma=False
    )
```

time: 261 us -> 46 us (0.18)
  waiting for transfers between devices: 80.4 us -> 0 us
  blocking collectives: 77.1 us -> 0 us
  Pallas kernels: 0 us -> 43.7 us
  other arithmetic: 37.5 us -> 0 us
  local copies, waits for them, and re-layouts: 20.5 us -> 1.39 us
  starting transfers between devices: 18.2 us -> 0 us
  between operations: 14.2 us -> 0.66 us
  matrix products: 8.65 us -> 0 us
  loops' own time: 3.05 us -> 0 us
    all_gather x1 -> x0, waiting for transfers between devices: 64.9 us -> none  [combined_all(): pieces = jax.tree.map(lambda part: lax.all_gather(part, axis), value)]
    all_gather x3 -> x0, blocking collectives: 59.2 us -> none  [the longest x2 31.5 us: combined_all(): pieces = jax.tree.map(lambda part: lax.all_gather(part, axis), value)]
    pallas_call x0 -> x1, Pallas kernels: none -> 43.7 us  [shards(): pl.pallas_call(kernel, out_shape=jax.ShapeDtypeStruct((TOK, HEADS * HD),...]
    add x39 -> x0, other arithmetic: 32.1 us -> none  [the longest x15 31.3 us: combine(): output = left[2] * scale_left[..., None] + right[2] * scale_right[..., None]]
    all_to_all x3 -> x0, starting transfers between devices: 18.2 us -> none  [the longest x1 10.5 us: shards(): lax.all_to_all(rotated, 'head', split_axis=1, concat_axis=0, tiled=True)]
    all_to_all x1 -> x0, blocking collectives: 17.9 us -> none  [shards(): lax.all_to_all(result, 'head', split_axis=0, concat_axis=1, tiled=True)]
    all_to_all x3 -> x0, waiting for transfers between devices: 15.4 us -> none  [the longest x1 8.68 us: shards(): lax.all_to_all(keys_wide, 'head', split_axis=1, concat_axis=0, tiled=True)]
    slice x3 -> x0, local copies, waits for them, and re-layouts: 12.4 us -> none  [combined_all(): tail = jax.tree.map(lambda part: part[1:], pieces)]
  transfers between devices with their start and end apart: 4 -> 0, of which waited for: 3 -> 0; matrix products, arithmetic and copies ran while one was open for 1% -> 0% of each run, Pallas kernels for 0% -> 0%
where the time goes in v1:
time: 46 us; the launch traced here: 45.7 us
  Pallas kernels  43.7 us (95%)
  local copies, waits for them, and re-layouts  1.39 us (3%)
  between operations  0.66 us (1%)
    pallas_call x1, Pallas kernels, shards(): pl.pallas_call(kernel, out_shape=jax.ShapeDtypeStruct((TOK, HEADS * HD),...  43.7 us
    unnamed x1, local copies, waits for them, and re-layouts  1.39 us

profile of v1, /device:TPU:1, one launch (start us, length us, event | category | flops | bytes accessed | tf_op | source)
XLA Modules:
  0.0 45.7 jit_solution(5801981640742843793)
XLA Ops:
  0.7 43.7 %shard_map.73 = bf16[4,4096]{1,0:T(4,128)(2,1)} custom-call(s32[1]{0:T(128)S(6)} %copy.9.start_ref, f32[1,128]{1,0:T(1,128)} %constant.2.clone.freq_ref, bf16[4,4096]{1,0:T(4,128)(2,1)} %q_ref.1, bf16[4,1024]{1,0:T(4,128)(2,1)} %k_ref.1, bf16[4,1024]{1,0:T(4,128)(2,1)} %v_ref.1, bf16[8,1024,128]{2,1,0:T(8,128)(2,1)} %ck_ref.1, bf16[8,1024,128]{2,1,0:T(8,128)(2,1)} %cv_ref.1), custom_call_target="tpu_custom_call" | custom-call | tf_op jit(solution)/shard_map/pallas_call | solution.py:271
  44.3 1.4 %copy.10 = bf16[4,4096]{1,0:T(4,128)(2,1)} copy(bf16[4,4096]{1,0:T(4,128)(2,1)} %shard_map.73) | data formatting | bytes 65536

commit v2 on v1

v2 whole, which is shorter than its diff:
```python
import functools
import math

import jax
import jax.numpy as jnp
import numpy as np
from jax import lax
from jax.experimental import pallas as pl
from jax.experimental.pallas import tpu as pltpu
from jax.sharding import PartitionSpec as P

HEADS = 32
KVH = 8
HD = 128
GROUP = HEADS // KVH
THETA = 500000.0
MESH = pl.DeviceIdType.MESH

NX, NY, NZ, NC = 4, 8, 8, 2
NG = NX * NC
TOK = 4
ROWS = TOK * GROUP
CHUNK = NG * ROWS
EXP_SCALE = HD ** (-0.5) * math.log2(math.e)


def frequencies():
    half = HD // 2
    base = THETA ** (-(np.arange(half, dtype=np.float64) * 2.0 / HD))
    wave = 2.0 * np.pi / base
    smooth = (8192.0 / wave - 1.0) / 3.0
    blended = (1.0 - smooth) * base / 8.0 + smooth * base
    freq = np.where(wave < 2048.0, base, np.where(wave > 8192.0, base / 8.0, blended))
    return np.concatenate([freq, freq]).astype(np.float32)[None, :]


def kernel(
    start_hbm, freq_hbm, q_hbm, k_hbm, v_hbm, ck_ref, cv_ref, o_ref,
    start_ref, freq_ref, q_ref, k_ref, v_ref,
    sq, skv, qall, kvall, kbuf, vbuf, acc, low, tot, so, ss, ro, rs, sf,
    isem, csem, xsend, xrecv, qsend, qrecv, fsend, frecv, osend, orecv, ssend, srecv, rsend, rrecv,
):
    cached = ck_ref.shape[1]
    old = 2 * cached
    fresh = NY * NG * TOK
    head, kv = lax.axis_index("head"), lax.axis_index("kv")
    x, y = lax.div(head, NY), lax.rem(head, NY)
    z, c = lax.div(kv, NC), lax.rem(kv, NC)
    g = x * NC + c

    def of_group(other):
        return (lax.div(other, NC) * NY + y, z * NC + lax.rem(other, NC))

    def of_plane(other):
        return (head, other * NC + c)

    def of_row(other):
        return (x * NY + other, kv)

    groups = [lax.rem(g + i, NG) for i in range(1, NG)]
    planes = [lax.rem(z + i, NZ) for i in (1, 7, 2, 6, 3, 5, 4)]
    rows = [lax.rem(y + i, NY) for i in (4, 3, 5, 2, 6, 1, 7)]

    barrier = pltpu.get_barrier_semaphore()
    peers = [of_group(i) for i in groups] + [of_plane(i) for i in planes] + [of_row(i) for i in rows]
    for peer in peers:
        pl.semaphore_signal(barrier, inc=1, device_id=peer, device_id_type=MESH)

    inputs = [
        pltpu.make_async_copy(source, target, isem.at[i])
        for i, (source, target) in enumerate(
            (
                (start_hbm, start_ref), (freq_hbm, freq_ref), (q_hbm, q_ref), (k_hbm, k_ref),
                (v_hbm, v_ref),
            )
        )
    ]
    for copy in inputs:
        copy.start()
    own_k = pltpu.make_async_copy(ck_ref.at[g], kbuf.at[pl.ds(0, cached)], csem.at[0])
    own_v = pltpu.make_async_copy(cv_ref.at[g], vbuf.at[pl.ds(0, cached)], csem.at[1])
    own_k.start()
    own_v.start()
    for copy in inputs:
        copy.wait()

    first = start_ref[0] + (head * (NZ * NC) + kv) * TOK
    places = first + lax.broadcasted_iota(jnp.int32, (TOK, HD), 0)
    angle = places.astype(jnp.float32) * freq_ref[...]
    lane = lax.broadcasted_iota(jnp.int32, (TOK, HD), 1)
    cosine = jnp.cos(angle)
    sine = jnp.sin(angle)
    sine = jnp.where(lane < HD // 2, -sine, sine)
    cos_q = jnp.concatenate([cosine] * GROUP, 0)
    sin_q = jnp.concatenate([sine] * GROUP, 0)
    for i in range(NG):
        part = jnp.concatenate(
            [
                q_ref[:, (i * GROUP + j) * HD : (i * GROUP + j + 1) * HD].astype(jnp.float32)
                for j in range(GROUP)
            ],
            0,
        )
        turned = part * cos_q + pltpu.roll(part, HD // 2, 1) * sin_q
        sq[i] = turned.astype(jnp.bfloat16)
        part = k_ref[:, i * HD : (i + 1) * HD].astype(jnp.float32)
        turned = part * cosine + pltpu.roll(part, HD // 2, 1) * sine
        value = v_ref[:, i * HD : (i + 1) * HD].astype(jnp.float32)
        skv[i] = jnp.concatenate([turned, value], 0).astype(jnp.bfloat16)

    pl.semaphore_wait(barrier, len(peers))

    sends = []

    def send(source, target, sent, got, device):
        copy = pltpu.make_async_remote_copy(
            src_ref=source, dst_ref=target, send_sem=sent, recv_sem=got,
            device_id=device, device_id_type=MESH,
        )
        copy.start()
        sends.append(copy)

    def landed(target, got):
        pltpu.make_async_copy(target, target, got).wait()

    partner = x * NC + (1 - c)
    for i in groups:
        send(sq.at[i], qall.at[z, g], xsend.at[0, i], xrecv.at[0, g], of_group(i))
    for i in groups:
        send(skv.at[i], kvall.at[y, g], xsend.at[1, i], xrecv.at[1, g], of_group(i))
    for i, (source, target) in enumerate(((ck_ref, kbuf), (cv_ref, vbuf))):
        half = target.at[pl.ds(cached, cached)]
        send(source.at[partner], half, csem.at[2 + i], csem.at[4 + i], of_group(partner))
    qall[z, g] = sq[g]
    kvall[y, g] = skv[g]

    for i in groups:
        landed(qall.at[z, i], xrecv.at[0, i])
    for i in planes:
        send(qall.at[z], qall.at[z], qsend.at[i], qrecv.at[z], of_plane(i))
    for i in groups:
        landed(kvall.at[y, i], xrecv.at[1, i])
    for i in rows:
        send(kvall.at[y], kvall.at[y], fsend.at[i], frecv.at[y], of_row(i))

    own_k.wait()
    own_v.wait()
    for i, target in enumerate((kbuf, vbuf)):
        landed(target.at[pl.ds(cached, cached)], csem.at[4 + i])

    wide = 2 * CHUNK
    square = (CHUNK, CHUNK)
    diagonal = lax.broadcasted_iota(jnp.int32, square, 0) == lax.broadcasted_iota(
        jnp.int32, square, 1
    )

    def pair_of(i):
        return (lax.rem(z - i + NZ, NZ), lax.rem(z + i + 1, NZ))

    def queries_of(pair):
        return jnp.concatenate([qall[one].reshape(CHUNK, HD) for one in pair], 0)

    def scores_of(queries, keys):
        return lax.dot_general(
            queries, keys, (((1,), (1,)), ((), ())), preferred_element_type=jnp.float32
        )

    def weigh(probs, values):
        ones = jnp.ones(values.shape, jnp.bfloat16)
        both = jnp.dot(
            probs, jnp.concatenate([values, ones], 1), preferred_element_type=jnp.float32
        )
        return both[:, :HD], both[:, HD:]

    def await_pair(i, pair):
        @pl.when(i > 0)
        def _():
            landed(qall.at[pair[0]], qrecv.at[pair[0]])

        landed(qall.at[pair[1]], qrecv.at[pair[1]])

    def on_cached(i, carry):
        pair = pair_of(i)
        await_pair(i, pair)
        scores = scores_of(queries_of(pair), kbuf[:old])
        top = jnp.max(scores, 1, keepdims=True) * EXP_SCALE
        probs = jnp.exp2(scores * EXP_SCALE - top).astype(jnp.bfloat16)
        output, total = weigh(probs, vbuf[:old])
        acc[i] = output
        tot[i] = total
        low[i] = jnp.broadcast_to(top, (wide, HD))
        return carry

    lax.fori_loop(0, 2, on_cached, 0)

    for i in rows:
        landed(kvall.at[i], frecv.at[i])
    for i in range(NY):
        for j in range(NG // 4):
            four = [kvall[i, j * 4 + n].astype(jnp.float32) for n in range(4)]
            place = old + (i * NG + j * 4) * TOK
            kbuf[place : place + 16] = jnp.concatenate(
                [one[:TOK] for one in four], 0
            ).astype(jnp.bfloat16)
            vbuf[place : place + 16] = jnp.concatenate(
                [one[TOK:] for one in four], 0
            ).astype(jnp.bfloat16)

    row = lax.broadcasted_iota(jnp.int32, (wide, fresh), 0)
    column = lax.broadcasted_iota(jnp.int32, (wide, fresh), 1)
    row_group = lax.rem(lax.div(row, ROWS), NG)
    row_token = (lax.div(row_group, NC) * NY + y) * (NZ * NC * TOK) + (
        lax.rem(row_group, NC) * TOK + lax.rem(row, TOK)
    )
    column_group = lax.rem(lax.div(column, TOK), NG)
    column_token = (
        lax.div(column_group, NC) * NY + lax.div(column, NG * TOK)
    ) * (NZ * NC * TOK) + (lax.rem(column_group, NC) * TOK + lax.rem(column, TOK))
    behind = row_token - column_token - z * (NC * TOK)

    def hide(scores, pair):
        plane = jnp.where(row < CHUNK, pair[0], pair[1]) * (NC * TOK)
        return jnp.where(behind + plane >= 0, scores, -1e30)

    def give(i, pair, output, total, top):
        level = top + jnp.log2(total)
        output = (output / total).astype(jnp.bfloat16)
        for n in range(2):
            part = slice(n * CHUNK, (n + 1) * CHUNK)
            so[pair[n]] = output[part]
            ss[pair[n]] = jnp.sum(jnp.where(diagonal, level[part], 0.0), 0, keepdims=True)

        def one(other):
            for source, target, sent, got in ((so, ro, osend, orecv), (ss, rs, ssend, srecv)):
                pltpu.make_async_remote_copy(
                    src_ref=source.at[other], dst_ref=target.at[z], send_sem=sent.at[other],
                    recv_sem=got.at[z], device_id=of_plane(other), device_id_type=MESH,
                ).start()

        @pl.when(i > 0)
        def _():
            one(pair[0])

        one(pair[1])

    def on_new(i, carry):
        pair = pair_of(i)
        scores = hide(scores_of(queries_of(pair), kbuf[old:]), pair)
        before = low[i]
        top = jnp.maximum(before, jnp.max(scores, 1, keepdims=True) * EXP_SCALE)
        both = jnp.concatenate([top] * (fresh // HD), 1)
        probs = jnp.exp2(scores * EXP_SCALE - both).astype(jnp.bfloat16)
        output, total = weigh(probs, vbuf[old:])
        keep = jnp.exp2(before - top)
        give(i, pair, acc[i] * keep + output, tot[i] * keep + total, top)
        return carry

    lax.fori_loop(0, 2, on_new, 0)

    def on_all(i, carry):
        pair = pair_of(i)
        await_pair(i, pair)
        scores = scores_of(queries_of(pair), kbuf[...])
        scores = jnp.concatenate([scores[:, :old], hide(scores[:, old:], pair)], 1)
        top = jnp.max(scores, 1, keepdims=True) * EXP_SCALE
        probs = jnp.exp2(scores * EXP_SCALE - top).astype(jnp.bfloat16)
        output, total = weigh(probs, vbuf[...])
        give(i, pair, output, total, top)
        return carry

    lax.fori_loop(2, NZ // 2, on_all, 0)
    ro[z] = so[z]
    rs[z] = ss[z]

    for i in planes:
        landed(rs.at[i], srecv.at[i])
        landed(ro.at[i], orecv.at[i])
    levels = rs[:, 0, :]
    weight = jnp.exp2(levels - jnp.max(levels, 0, keepdims=True))
    weight = weight / jnp.sum(weight, 0, keepdims=True)
    weight = jnp.transpose(weight)
    total = weight[:, 0:1] * ro[0].astype(jnp.float32)
    for i in range(1, NZ):
        total = total + weight[:, i : i + 1] * ro[i].astype(jnp.float32)
    for i in range(NG):
        for j in range(GROUP):
            place = i * ROWS + j * TOK
            sf[i, :, j * HD : (j + 1) * HD] = total[place : place + TOK].astype(jnp.bfloat16)
    width = GROUP * HD
    place = pl.ds(pl.multiple_of(g * width, width), width)
    for i in groups:
        send(sf.at[i], o_ref.at[:, place], rsend.at[i], rrecv.at[g], of_group(i))
    own = pltpu.make_async_copy(sf.at[g], o_ref.at[:, place], rsend.at[g])
    own.start()
    for copy in sends:
        copy.wait_send()
    for i in planes:
        for source, sent in ((so, osend), (ss, ssend)):
            landed(source.at[i], sent.at[i])
    own.wait()
    for i in groups:
        landed(o_ref.at[:, pl.ds(pl.multiple_of(i * width, width), width)], rrecv.at[i])


def shards(queries, new_keys, new_values, cache_keys, cache_values, start):
    cached = cache_keys.shape[1]
    keys = 2 * cached + NY * NG * TOK
    hbm = pl.BlockSpec(memory_space=pltpu.HBM)
    dma = pltpu.SemaphoreType.DMA
    bf16 = jnp.bfloat16
    return pl.pallas_call(
        kernel,
        out_shape=jax.ShapeDtypeStruct((TOK, HEADS * HD), bf16),
        in_specs=[hbm] * 7,
        out_specs=hbm,
        scratch_shapes=[
            pltpu.SMEM((1,), jnp.int32),
            pltpu.VMEM((1, HD), jnp.float32),
            pltpu.VMEM((TOK, HEADS * HD), bf16),
            pltpu.VMEM((TOK, KVH * HD), bf16),
            pltpu.VMEM((TOK, KVH * HD), bf16),
            pltpu.VMEM((NG, ROWS, HD), bf16),
            pltpu.VMEM((NG, 2 * TOK, HD), bf16),
            pltpu.VMEM((NZ, NG, ROWS, HD), bf16),
            pltpu.VMEM((NY, NG, 2 * TOK, HD), bf16),
            pltpu.VMEM((keys, HD), bf16),
            pltpu.VMEM((keys, HD), bf16),
            pltpu.VMEM((2, 2 * CHUNK, HD), jnp.float32),
            pltpu.VMEM((2, 2 * CHUNK, HD), jnp.float32),
            pltpu.VMEM((2, 2 * CHUNK, HD), jnp.float32),
            pltpu.VMEM((NZ, CHUNK, HD), bf16),
            pltpu.VMEM((NZ, 1, CHUNK), jnp.float32),
            pltpu.VMEM((NZ, CHUNK, HD), bf16),
            pltpu.VMEM((NZ, 1, CHUNK), jnp.float32),
            pltpu.VMEM((NG, TOK, GROUP * HD), bf16),
            dma((5,)), dma((6,)), dma((2, NG)), dma((2, NG)), dma((NZ,)), dma((NZ,)), dma((NY,)), dma((NY,)),
            dma((NZ,)), dma((NZ,)), dma((NZ,)), dma((NZ,)), dma((NG,)), dma((NG,)),
        ],
        compiler_params=pltpu.CompilerParams(
            collective_id=0, has_side_effects=True, vmem_limit_bytes=60000 * 1024
        ),
    )(start, jnp.asarray(frequencies()), queries, new_keys, new_values, cache_keys, cache_values)


def solution(mesh):
    placed = (
        P(("head", "kv"), None),
        P(("head", "kv"), None),
        P(("head", "kv"), None),
        P(None, "kv", None),
        P(None, "kv", None),
        P(),
    )
    return jax.shard_map(
        shards, mesh=mesh, in_specs=placed, out_specs=P(("head", "kv"), None), check_vma=False
    )
```

time: 46 us -> 44.1 us (0.959)
  Pallas kernels: 43.7 us -> 41.9 us
    pallas_call x1, Pallas kernels: 43.7 us -> 41.9 us  [shards(): pl.pallas_call(kernel, out_shape=jax.ShapeDtypeStruct((TOK, HEADS * HD),...]
where the time goes in v2:
time: 44.1 us; the launch traced here: 43.9 us
  Pallas kernels  41.9 us (95%)
  local copies, waits for them, and re-layouts  1.39 us (3%)
  between operations  0.66 us (1%)
    pallas_call x1, Pallas kernels, shards(): pl.pallas_call(kernel, out_shape=jax.ShapeDtypeStruct((TOK, HEADS * HD),...  41.9 us
    unnamed x1, local copies, waits for them, and re-layouts  1.39 us

profile of v2, /device:TPU:1, one launch (start us, length us, event | category | flops | bytes accessed | tf_op | source)
XLA Modules:
  0.0 43.9 jit_solution(2249725004567856857)
XLA Ops:
  0.7 41.9 %shard_map.73 = bf16[4,4096]{1,0:T(4,128)(2,1)} custom-call(s32[1]{0:T(128)S(6)} %copy.9.start_hbm, f32[1,128]{1,0:T(1,128)} %constant.2.clone.freq_hbm, bf16[4,4096]{1,0:T(4,128)(2,1)} %q_hbm.1, bf16[4,1024]{1,0:T(4,128)(2,1)} %k_hbm.1, bf16[4,1024]{1,0:T(4,128)(2,1)} %v_hbm.1, bf16[8,1024,128]{2,1,0:T(8,128)(2,1)} %ck_ref.1, bf16[8,1024,128]{2,1,0:T(8,128)(2,1)} %cv_ref.1), custom_call_target="tpu_custom_call" | custom-call | tf_op jit(solution)/shard_map/pallas_call | solution.py:311
  42.5 1.4 %copy.10 = bf16[4,4096]{1,0:T(4,128)(2,1)} copy(bf16[4,4096]{1,0:T(4,128)(2,1)} %shard_map.73) | data formatting | bytes 65536

commit v3 on v2

v3 whole, which is shorter than its diff:
```python
import math

import jax
import jax.numpy as jnp
import numpy as np
from jax import lax
from jax.experimental import pallas as pl
from jax.experimental.pallas import tpu as pltpu
from jax.sharding import PartitionSpec as P

HEADS = 32
KVH = 8
HD = 128
GROUP = HEADS // KVH
THETA = 500000.0
MESH = pl.DeviceIdType.MESH

NX, NY, NZ, NC = 4, 8, 8, 2
NG = NX * NC
NS = NZ * NC
OWN = KVH // NC
TOK = 4
ROWS = TOK * GROUP
ALL = NS * ROWS
FRESH = NY * NG * TOK
EXP_SCALE = HD ** (-0.5) * math.log2(math.e)
ORDER = (0, 1, 7, 2, 6, 3, 5, 4)
PLACE = tuple(ORDER.index(i) for i in range(8))
PIECES = 2
PART = NY // PIECES


def frequencies():
    half = HD // 2
    base = THETA ** (-(np.arange(half, dtype=np.float64) * 2.0 / HD))
    wave = 2.0 * np.pi / base
    smooth = (8192.0 / wave - 1.0) / 3.0
    blended = (1.0 - smooth) * base / 8.0 + smooth * base
    freq = np.where(wave < 2048.0, base, np.where(wave > 8192.0, base / 8.0, blended))
    return np.concatenate([freq, freq]).astype(np.float32)[None, :]


def kernel(
    start_hbm, freq_hbm, q_hbm, k_hbm, v_hbm, ck_ref, cv_ref, o_ref,
    start_ref, freq_ref, q_ref, k_ref, v_ref,
    sq, qall, ybuf, piece, kvb, acc, low, tot, so, ss, ro, rs, turn, out,
    isem, csem, qsend, qrecv, ysend, yrecv, xsend, xrecv, osend, orecv, ssend, srecv,
):
    cached = ck_ref.shape[1]
    old = 2 * cached
    head, kv = lax.axis_index("head"), lax.axis_index("kv")
    x, y = lax.div(head, NY), lax.rem(head, NY)
    z, c = lax.div(kv, NC), lax.rem(kv, NC)
    g = x * NC + c
    mine, theirs = c * OWN, (1 - c) * OWN

    def of_row(other):
        return (lax.div(other, NC) * NY + y, z * NC + lax.rem(other, NC))

    column = [lax.rem(z + d, NZ) * NC + n for d in ORDER[1:] for n in range(NC)]
    partner = z * NC + (1 - c)
    column = [partner] + column
    ring = [lax.rem(y + d, NY) for d in ORDER[1:]]
    row = [lax.rem(g + i, NG) for i in range(1, NG)]

    barrier = pltpu.get_barrier_semaphore()
    peers = (
        [(head, i) for i in column] + [(x * NY + i, kv) for i in ring] + [of_row(i) for i in row]
    )
    for device in peers:
        pl.semaphore_signal(barrier, inc=1, device_id=device, device_id_type=MESH)

    inputs = [
        pltpu.make_async_copy(source, target, isem.at[i])
        for i, (source, target) in enumerate(
            (
                (start_hbm, start_ref), (freq_hbm, freq_ref), (q_hbm, q_ref), (k_hbm, k_ref),
                (v_hbm, v_ref),
            )
        )
    ]
    for copy in inputs:
        copy.start()
    caches = []
    for i, source in enumerate((ck_ref, cv_ref)):
        copy = pltpu.make_async_copy(
            source.at[pl.ds(mine, OWN)], kvb.at[i, :, pl.ds(0, cached)], csem.at[i]
        )
        copy.start()
        caches.append(copy)
    for copy in inputs:
        copy.wait()

    first = start_ref[0] + (head * NS + kv) * TOK
    places = first + lax.broadcasted_iota(jnp.int32, (TOK, HD), 0)
    angle = places.astype(jnp.float32) * freq_ref[...]
    lane = lax.broadcasted_iota(jnp.int32, (TOK, HD), 1)
    cosine = jnp.cos(angle)
    sine = jnp.sin(angle)
    sine = jnp.where(lane < HD // 2, -sine, sine)
    cos_q = jnp.concatenate([cosine] * GROUP, 0)
    sin_q = jnp.concatenate([sine] * GROUP, 0)
    for i in range(KVH):
        part = jnp.concatenate(
            [
                q_ref[:, (i * GROUP + j) * HD : (i * GROUP + j + 1) * HD].astype(jnp.float32)
                for j in range(GROUP)
            ],
            0,
        )
        turned = part * cos_q + pltpu.roll(part, HD // 2, 1) * sin_q
        sq[i] = turned.astype(jnp.bfloat16)
        part = k_ref[:, i * HD : (i + 1) * HD].astype(jnp.float32)
        turned = part * cosine + pltpu.roll(part, HD // 2, 1) * sine
        value = v_ref[:, i * HD : (i + 1) * HD].astype(jnp.float32)
        ybuf[0, i] = jnp.concatenate([turned, value], 0).astype(jnp.bfloat16)

    pl.semaphore_wait(barrier, len(peers))

    sends = []

    def send(source, target, sent, got, device):
        copy = pltpu.make_async_remote_copy(
            src_ref=source, dst_ref=target, send_sem=sent, recv_sem=got,
            device_id=device, device_id_type=MESH,
        )
        copy.start()
        sends.append(copy)

    def landed(target, got):
        pltpu.make_async_copy(target, target, got).wait()

    for i in column:
        half = sq.at[pl.ds(lax.rem(i, NC) * OWN, OWN)]
        send(half, qall.at[:, kv], qsend.at[i], qrecv.at[kv], (head, i))
    for d, i in zip(ORDER[1:], ring):
        place = PLACE[(NY - d) % NY]
        send(ybuf.at[0], ybuf.at[place], ysend.at[place], yrecv.at[place], (x * NY + i, kv))
    for i, source in enumerate((ck_ref, cv_ref)):
        send(
            source.at[pl.ds(theirs, OWN)], kvb.at[i, :, pl.ds(cached, cached)],
            csem.at[2 + i], csem.at[4 + i], (head, partner),
        )
    for j in range(OWN):
        qall[j, kv] = sq[mine + j]

    for m in range(PIECES):
        for i in range(m * PART, (m + 1) * PART):
            if i > 0:
                landed(ybuf.at[i], yrecv.at[i])
        for j in range(KVH):
            four = [ybuf[m * PART + n, j].astype(jnp.float32) for n in range(PART)]
            piece[m, 0, j] = jnp.concatenate([one[:TOK] for one in four], 0).astype(jnp.bfloat16)
            piece[m, 1, j] = jnp.concatenate([one[TOK:] for one in four], 0).astype(jnp.bfloat16)
        size = PART * TOK
        there = pl.ds(pl.multiple_of(old + (g * PIECES + m) * size, size), size)
        for i in row:
            half = piece.at[m, :, pl.ds(lax.rem(i, NC) * OWN, OWN)]
            send(half, kvb.at[:, :, there], xsend.at[m, i], xrecv.at[m, g], of_row(i))
        for j in range(OWN):
            kvb[0, j, there] = piece[m, 0, mine + j]
            kvb[1, j, there] = piece[m, 1, mine + j]

    for i, copy in enumerate(caches):
        copy.wait()
        landed(kvb.at[i, :, pl.ds(cached, cached)], csem.at[4 + i])
    for i in column:
        landed(qall.at[:, i], qrecv.at[i])

    def scores_of(j, keys):
        return lax.dot_general(
            qall[j].reshape(ALL, HD), keys, (((1,), (1,)), ((), ())),
            preferred_element_type=jnp.float32,
        )

    def weigh(probs, values):
        ones = jnp.ones(values.shape, jnp.bfloat16)
        both = jnp.dot(
            probs, jnp.concatenate([values, ones], 1), preferred_element_type=jnp.float32
        )
        return both[:, :HD], both[:, HD:]

    def on_cached(j, carry):
        scores = scores_of(j, kvb[0, j, :old])
        top = jnp.max(scores, 1, keepdims=True) * EXP_SCALE
        probs = jnp.exp2(scores * EXP_SCALE - top).astype(jnp.bfloat16)
        output, total = weigh(probs, kvb[1, j, :old])
        acc[j] = output
        tot[j] = total
        low[j] = jnp.broadcast_to(top, (ALL, HD))
        return carry

    lax.fori_loop(0, OWN, on_cached, 0)

    for m in range(PIECES):
        size = PART * TOK
        for i in row:
            there = pl.ds(pl.multiple_of(old + (i * PIECES + m) * size, size), size)
            landed(kvb.at[:, :, there], xrecv.at[m, i])

    at_row = lax.broadcasted_iota(jnp.int32, (ALL, FRESH), 0)
    at_key = lax.broadcasted_iota(jnp.int32, (ALL, FRESH), 1)
    row_token = (head * NS + lax.div(at_row, ROWS)) * TOK + lax.rem(at_row, TOK)
    source = lax.div(at_key, NY * TOK)
    place = lax.rem(lax.div(at_key, TOK), NY)
    away = lax.div(place + 1, 2)
    away = jnp.where(lax.rem(place, 2) == 1, away, NY - away)
    key_head = lax.div(source, NC) * NY + lax.rem(y + away, NY)
    key_token = (key_head * NS + z * NC + lax.rem(source, NC)) * TOK + lax.rem(at_key, TOK)
    visible = key_token <= row_token
    square = (CHUNK, CHUNK)
    diagonal = lax.broadcasted_iota(jnp.int32, square, 0) == lax.broadcasted_iota(
        jnp.int32, square, 1
    )

    for j in range(OWN):
        scores = jnp.where(visible, scores_of(j, kvb[0, j, old:]), -1e30)
        before = low[j]
        top = jnp.maximum(before, jnp.max(scores, 1, keepdims=True) * EXP_SCALE)
        both = jnp.concatenate([top] * (FRESH // HD), 1)
        probs = jnp.exp2(scores * EXP_SCALE - both).astype(jnp.bfloat16)
        output, total = weigh(probs, kvb[1, j, old:])
        keep = jnp.exp2(before - top)
        output = acc[j] * keep + output
        total = tot[j] * keep + total
        level = top + jnp.log2(total)
        output = (output / total).astype(jnp.bfloat16)
        so[:, j] = output.reshape(NS, ROWS, HD)
        for n in range(HALVES):
            part = level[n * CHUNK : (n + 1) * CHUNK]
            ss[n, j : j + 1, :] = jnp.sum(jnp.where(diagonal, part, 0.0), 0, keepdims=True)
        if j % 2 == 1:
            two = pl.ds(j - 1, 2)
            for i in column:
                send(
                    so.at[i, two], ro.at[kv, two], osend.at[j // 2, i], orecv.at[j // 2, kv],
                    (head, i),
                )
    for i in column:
        send(ss.at[lax.div(i, NS // HALVES)], rs.at[kv], ssend.at[i], srecv.at[kv], (head, i))
    ro[kv] = so[kv]
    rs[kv] = ss[lax.div(kv, NS // HALVES)]

    for i in column:
        landed(rs.at[i], srecv.at[i])
    levels = jnp.concatenate(
        [rs[:, j : j + 1, :].reshape(NZ, NC, CHUNK) for j in range(OWN)], 1
    )
    weight = jnp.exp2(levels - jnp.max(levels, 0, keepdims=True))
    weight = weight / jnp.sum(weight, 0, keepdims=True)
    turn[...] = jnp.transpose(weight.reshape(NZ * KVH, CHUNK))
    begin = pl.multiple_of(lax.rem(kv, NS // HALVES) * ROWS, ROWS)
    weight = turn[pl.ds(begin, ROWS), :]
    for i in column:
        for m in range(OWN // 2):
            two = pl.ds(2 * m, 2)
            landed(ro.at[i, two], orecv.at[m, i])
    for n in range(NC):
        for j in range(OWN):
            total = jnp.zeros((ROWS, HD), jnp.float32)
            for i in range(NZ):
                at = i * KVH + j * NC + n
                total = total + weight[:, at : at + 1] * ro[i * NC + n, j].astype(jnp.float32)
            for h in range(GROUP):
                at = ((n * OWN + j) * GROUP + h) * HD
                out[:, at : at + HD] = total[h * TOK : (h + 1) * TOK].astype(jnp.bfloat16)
    done = pltpu.make_async_copy(out, o_ref, isem.at[0])
    done.start()
    for copy in sends:
        copy.wait_send()
    done.wait()


HALVES = 2
CHUNK = ALL // HALVES


def shards(queries, new_keys, new_values, cache_keys, cache_values, start):
    keys = 2 * cache_keys.shape[1] + FRESH
    hbm = pl.BlockSpec(memory_space=pltpu.HBM)
    dma = pltpu.SemaphoreType.DMA
    bf16 = jnp.bfloat16
    f32 = jnp.float32
    return pl.pallas_call(
        kernel,
        out_shape=jax.ShapeDtypeStruct((TOK, HEADS * HD), bf16),
        in_specs=[hbm] * 7,
        out_specs=hbm,
        scratch_shapes=[
            pltpu.SMEM((1,), jnp.int32),
            pltpu.VMEM((1, HD), f32),
            pltpu.VMEM((TOK, HEADS * HD), bf16),
            pltpu.VMEM((TOK, KVH * HD), bf16),
            pltpu.VMEM((TOK, KVH * HD), bf16),
            pltpu.VMEM((KVH, ROWS, HD), bf16),
            pltpu.VMEM((OWN, NS, ROWS, HD), bf16),
            pltpu.VMEM((NY, KVH, 2 * TOK, HD), bf16),
            pltpu.VMEM((PIECES, 2, KVH, PART * TOK, HD), bf16),
            pltpu.VMEM((2, OWN, keys, HD), bf16),
            pltpu.VMEM((OWN, ALL, HD), f32),
            pltpu.VMEM((OWN, ALL, HD), f32),
            pltpu.VMEM((OWN, ALL, HD), f32),
            pltpu.VMEM((NS, OWN, ROWS, HD), bf16),
            pltpu.VMEM((HALVES, OWN, CHUNK), f32),
            pltpu.VMEM((NS, OWN, ROWS, HD), bf16),
            pltpu.VMEM((NS, OWN, CHUNK), f32),
            pltpu.VMEM((CHUNK, NZ * KVH), f32),
            pltpu.VMEM((TOK, HEADS * HD), bf16),
            dma((5,)), dma((6,)), dma((NS,)), dma((NS,)), dma((NY,)), dma((NY,)),
            dma((PIECES, NG)), dma((PIECES, NG)), dma((2, NS)), dma((2, NS)), dma((NS,)), dma((NS,)),
        ],
        compiler_params=pltpu.CompilerParams(
            collective_id=0, has_side_effects=True, vmem_limit_bytes=60000 * 1024
        ),
    )(start, jnp.asarray(frequencies()), queries, new_keys, new_values, cache_keys, cache_values)


def solution(mesh):
    placed = (
        P(("head", "kv"), None),
        P(("head", "kv"), None),
        P(("head", "kv"), None),
        P(None, "kv", None),
        P(None, "kv", None),
        P(),
    )
    return jax.shard_map(
        shards, mesh=mesh, in_specs=placed, out_specs=P(("head", "kv"), None), check_vma=False
    )
```

time: 44.1 us -> 43.3 us (0.982)
  Pallas kernels: 41.9 us -> 41 us
    pallas_call x1, Pallas kernels: 41.9 us -> 41 us  [shards(): pl.pallas_call(kernel, out_shape=jax.ShapeDtypeStruct((TOK, HEADS * HD),...]
where the time goes in v3:
time: 43.3 us; the launch traced here: 43.1 us
  Pallas kernels  41 us (95%)
  local copies, waits for them, and re-layouts  1.39 us (3%)
  between operations  0.66 us (2%)
    pallas_call x1, Pallas kernels, shards(): pl.pallas_call(kernel, out_shape=jax.ShapeDtypeStruct((TOK, HEADS * HD),...  41 us
    unnamed x1, local copies, waits for them, and re-layouts  1.39 us

profile of v3, /device:TPU:1, one launch (start us, length us, event | category | flops | bytes accessed | tf_op | source)
XLA Modules:
  0.0 43.1 jit_solution(11757933111277818037)
XLA Ops:
  0.7 41.0 %shard_map.73 = bf16[4,4096]{1,0:T(4,128)(2,1)} custom-call(s32[1]{0:T(128)S(6)} %copy.9.start_hbm, f32[1,128]{1,0:T(1,128)} %constant.2.clone.freq_hbm, bf16[4,4096]{1,0:T(4,128)(2,1)} %q_hbm.1, bf16[4,1024]{1,0:T(4,128)(2,1)} %k_hbm.1, bf16[4,1024]{1,0:T(4,128)(2,1)} %v_hbm.1, bf16[8,1024,128]{2,1,0:T(8,128)(2,1)} %ck_ref.1, bf16[8,1024,128]{2,1,0:T(8,128)(2,1)} %cv_ref.1), custom_call_target="tpu_custom_call" | custom-call | tf_op jit(solution)/shard_map/pallas_call | solution.py:284
  41.7 1.4 %copy.10 = bf16[4,4096]{1,0:T(4,128)(2,1)} copy(bf16[4,4096]{1,0:T(4,128)(2,1)} %shard_map.73) | data formatting | bytes 65536

commit v4 on v3

--- a/solution.py
+++ b/solution.py
@@ -28,6 +28,7 @@
 PLACE = tuple(ORDER.index(i) for i in range(8))
 PIECES = 2
 PART = NY // PIECES
+PAIR = 2
 
 
 def frequencies():
@@ -43,7 +44,7 @@
 def kernel(
     start_hbm, freq_hbm, q_hbm, k_hbm, v_hbm, ck_ref, cv_ref, o_ref,
     start_ref, freq_ref, q_ref, k_ref, v_ref,
-    sq, qall, ybuf, piece, kvb, acc, low, tot, so, ss, ro, rs, turn, out,
+    sq, qall, ybuf, piece, kvb, acc, low, tot, so, ss, ro, rs, out,
     isem, csem, qsend, qrecv, ysend, yrecv, xsend, xrecv, osend, orecv, ssend, srecv,
 ):
     cached = ck_ref.shape[1]
@@ -62,6 +63,7 @@
     column = [partner] + column
     ring = [lax.rem(y + d, NY) for d in ORDER[1:]]
     row = [lax.rem(g + i, NG) for i in range(1, NG)]
+    back = column[::-1]
 
     barrier = pltpu.get_barrier_semaphore()
     peers = (
@@ -144,7 +146,9 @@
     for j in range(OWN):
         qall[j, kv] = sq[mine + j]
 
-    for m in range(PIECES):
+    size = PART * TOK
+
+    def gather(m):
         for i in range(m * PART, (m + 1) * PART):
             if i > 0:
                 landed(ybuf.at[i], yrecv.at[i])
@@ -152,14 +156,25 @@
             four = [ybuf[m * PART + n, j].astype(jnp.float32) for n in range(PART)]
             piece[m, 0, j] = jnp.concatenate([one[:TOK] for one in four], 0).astype(jnp.bfloat16)
             piece[m, 1, j] = jnp.concatenate([one[TOK:] for one in four], 0).astype(jnp.bfloat16)
-        size = PART * TOK
-        there = pl.ds(pl.multiple_of(old + (g * PIECES + m) * size, size), size)
+
+    def rows_of(i, m):
+        return pl.ds(pl.multiple_of(old + (i * PIECES + m) * size, size), size)
+
+    def forward(h, m):
+        two = pl.ds(h * PAIR, PAIR)
         for i in row:
-            half = piece.at[m, :, pl.ds(lax.rem(i, NC) * OWN, OWN)]
-            send(half, kvb.at[:, :, there], xsend.at[m, i], xrecv.at[m, g], of_row(i))
-        for j in range(OWN):
-            kvb[0, j, there] = piece[m, 0, mine + j]
-            kvb[1, j, there] = piece[m, 1, mine + j]
+            half = piece.at[m, :, pl.ds(lax.rem(i, NC) * OWN + h * PAIR, PAIR)]
+            send(half, kvb.at[:, two, rows_of(g, m)], xsend.at[h, m, i], xrecv.at[h, m, g], of_row(i))
+        for j in range(h * PAIR, (h + 1) * PAIR):
+            for n in range(2):
+                kvb[n, j, rows_of(g, m)] = piece[m, n, mine + j]
+
+    gather(0)
+    forward(0, 0)
+    gather(1)
+    forward(0, 1)
+    forward(1, 0)
+    forward(1, 1)
 
     for i, copy in enumerate(caches):
         copy.wait()
@@ -189,14 +204,6 @@
         tot[j] = total
         low[j] = jnp.broadcast_to(top, (ALL, HD))
         return carry
-
-    lax.fori_loop(0, OWN, on_cached, 0)
-
-    for m in range(PIECES):
-        size = PART * TOK
-        for i in row:
-            there = pl.ds(pl.multiple_of(old + (i * PIECES + m) * size, size), size)
-            landed(kvb.at[:, :, there], xrecv.at[m, i])
 
     at_row = lax.broadcasted_iota(jnp.int32, (ALL, FRESH), 0)
     at_key = lax.broadcasted_iota(jnp.int32, (ALL, FRESH), 1)
@@ -208,59 +215,56 @@
     key_head = lax.div(source, NC) * NY + lax.rem(y + away, NY)
     key_token = (key_head * NS + z * NC + lax.rem(source, NC)) * TOK + lax.rem(at_key, TOK)
     visible = key_token <= row_token
-    square = (CHUNK, CHUNK)
-    diagonal = lax.broadcasted_iota(jnp.int32, square, 0) == lax.broadcasted_iota(
-        jnp.int32, square, 1
-    )
-
-    for j in range(OWN):
-        scores = jnp.where(visible, scores_of(j, kvb[0, j, old:]), -1e30)
-        before = low[j]
-        top = jnp.maximum(before, jnp.max(scores, 1, keepdims=True) * EXP_SCALE)
-        both = jnp.concatenate([top] * (FRESH // HD), 1)
-        probs = jnp.exp2(scores * EXP_SCALE - both).astype(jnp.bfloat16)
-        output, total = weigh(probs, kvb[1, j, old:])
-        keep = jnp.exp2(before - top)
-        output = acc[j] * keep + output
-        total = tot[j] * keep + total
-        level = top + jnp.log2(total)
-        output = (output / total).astype(jnp.bfloat16)
-        so[:, j] = output.reshape(NS, ROWS, HD)
-        for n in range(HALVES):
-            part = level[n * CHUNK : (n + 1) * CHUNK]
-            ss[n, j : j + 1, :] = jnp.sum(jnp.where(diagonal, part, 0.0), 0, keepdims=True)
-        if j % 2 == 1:
-            two = pl.ds(j - 1, 2)
-            for i in column:
-                send(
-                    so.at[i, two], ro.at[kv, two], osend.at[j // 2, i], orecv.at[j // 2, kv],
-                    (head, i),
-                )
-    for i in column:
-        send(ss.at[lax.div(i, NS // HALVES)], rs.at[kv], ssend.at[i], srecv.at[kv], (head, i))
+    lane_row = lax.broadcasted_iota(jnp.int32, (ALL, HD), 1) - lax.rem(
+        lax.broadcasted_iota(jnp.int32, (ALL, HD), 0), ROWS
+    )
+
+    ss[...] = jnp.zeros_like(ss)
+    for h in range(OWN // PAIR):
+        lax.fori_loop(h * PAIR, (h + 1) * PAIR, on_cached, 0)
+        two = pl.ds(h * PAIR, PAIR)
+        for m in range(PIECES):
+            for i in row:
+                landed(kvb.at[:, two, rows_of(i, m)], xrecv.at[h, m, i])
+        for j in range(h * PAIR, (h + 1) * PAIR):
+            scores = jnp.where(visible, scores_of(j, kvb[0, j, old:]), -1e30)
+            before = low[j]
+            top = jnp.maximum(before, jnp.max(scores, 1, keepdims=True) * EXP_SCALE)
+            both = jnp.concatenate([top] * (FRESH // HD), 1)
+            probs = jnp.exp2(scores * EXP_SCALE - both).astype(jnp.bfloat16)
+            output, total = weigh(probs, kvb[1, j, old:])
+            keep = jnp.exp2(before - top)
+            output = acc[j] * keep + output
+            total = tot[j] * keep + total
+            level = top + jnp.log2(total)
+            output = (output / total).astype(jnp.bfloat16)
+            so[:, j] = output.reshape(NS, ROWS, HD)
+            level = jnp.where(lane_row == j * ROWS, level, 0.0).reshape(NS, ROWS, HD)
+            ss[...] += jnp.sum(level, 1, keepdims=True)
+        for i in back:
+            send(so.at[i, two], ro.at[kv, two], osend.at[h, i], orecv.at[h, kv], (head, i))
+    for i in back:
+        send(ss.at[i], rs.at[kv], ssend.at[i], srecv.at[kv], (head, i))
     ro[kv] = so[kv]
-    rs[kv] = ss[lax.div(kv, NS // HALVES)]
+    rs[kv] = ss[kv]
 
     for i in column:
         landed(rs.at[i], srecv.at[i])
-    levels = jnp.concatenate(
-        [rs[:, j : j + 1, :].reshape(NZ, NC, CHUNK) for j in range(OWN)], 1
-    )
+    levels = rs[:, 0, :].reshape(NZ, NC, HD)
     weight = jnp.exp2(levels - jnp.max(levels, 0, keepdims=True))
     weight = weight / jnp.sum(weight, 0, keepdims=True)
-    turn[...] = jnp.transpose(weight.reshape(NZ * KVH, CHUNK))
-    begin = pl.multiple_of(lax.rem(kv, NS // HALVES) * ROWS, ROWS)
-    weight = turn[pl.ds(begin, ROWS), :]
+    weight = jnp.transpose(weight.reshape(NS, HD))
     for i in column:
-        for m in range(OWN // 2):
-            two = pl.ds(2 * m, 2)
+        for m in range(OWN // PAIR):
+            two = pl.ds(m * PAIR, PAIR)
             landed(ro.at[i, two], orecv.at[m, i])
     for n in range(NC):
         for j in range(OWN):
             total = jnp.zeros((ROWS, HD), jnp.float32)
             for i in range(NZ):
-                at = i * KVH + j * NC + n
-                total = total + weight[:, at : at + 1] * ro[i * NC + n, j].astype(jnp.float32)
+                at = i * NC + n
+                share = weight[j * ROWS : (j + 1) * ROWS, at : at + 1]
+                total = total + share * ro[at, j].astype(jnp.float32)
             for h in range(GROUP):
                 at = ((n * OWN + j) * GROUP + h) * HD
                 out[:, at : at + HD] = total[h * TOK : (h + 1) * TOK].astype(jnp.bfloat16)
@@ -269,10 +273,6 @@
     for copy in sends:
         copy.wait_send()
     done.wait()
-
-
-HALVES = 2
-CHUNK = ALL // HALVES
 
 
 def shards(queries, new_keys, new_values, cache_keys, cache_values, start):
@@ -285,7 +285,7 @@
         kernel,
         out_shape=jax.ShapeDtypeStruct((TOK, HEADS * HD), bf16),
         in_specs=[hbm] * 7,
-        out_specs=hbm,
+        out_specs=pl.BlockSpec(memory_space=pl.ANY),
         scratch_shapes=[
             pltpu.SMEM((1,), jnp.int32),
             pltpu.VMEM((1, HD), f32),
@@ -301,18 +301,25 @@
             pltpu.VMEM((OWN, ALL, HD), f32),
             pltpu.VMEM((OWN, ALL, HD), f32),
             pltpu.VMEM((NS, OWN, ROWS, HD), bf16),
-            pltpu.VMEM((HALVES, OWN, CHUNK), f32),
+            pltpu.VMEM((NS, 1, HD), f32),
             pltpu.VMEM((NS, OWN, ROWS, HD), bf16),
-            pltpu.VMEM((NS, OWN, CHUNK), f32),
-            pltpu.VMEM((CHUNK, NZ * KVH), f32),
+            pltpu.VMEM((NS, 1, HD), f32),
             pltpu.VMEM((TOK, HEADS * HD), bf16),
             dma((5,)), dma((6,)), dma((NS,)), dma((NS,)), dma((NY,)), dma((NY,)),
-            dma((PIECES, NG)), dma((PIECES, NG)), dma((2, NS)), dma((2, NS)), dma((NS,)), dma((NS,)),
+            dma((2, PIECES, NG)), dma((2, PIECES, NG)), dma((2, NS)), dma((2, NS)), dma((NS,)), dma((NS,)),
         ],
         compiler_params=pltpu.CompilerParams(
-            collective_id=0, has_side_effects=True, vmem_limit_bytes=60000 * 1024
+            collective_id=0, has_side_effects=True, vmem_limit_bytes=40000 * 1024
         ),
-    )(start, jnp.asarray(frequencies()), queries, new_keys, new_values, cache_keys, cache_values)
+    )(
+        start,
+        *[
+            pltpu.with_memory_space_constraint(one, pltpu.HBM)
+            for one in (
+                jnp.asarray(frequencies()), queries, new_keys, new_values, cache_keys, cache_values
+            )
+        ],
+    )
 
 
 def solution(mesh):

time: 43.3 us -> 41.1 us (0.949)
  Pallas kernels: 41 us -> 39.7 us
  local copies, waits for them, and re-layouts: 1.39 us -> 0.62 us
    pallas_call x1, Pallas kernels: 41 us -> 39.7 us  [shards(): pl.pallas_call(kernel, out_shape=jax.ShapeDtypeStruct((TOK, HEADS * HD),...]
    unnamed x1, local copies, waits for them, and re-layouts: 1.39 us -> 0.62 us
where the time goes in v4:
time: 41.1 us; the launch traced here: 41 us
  Pallas kernels  39.7 us (97%)
  between operations  0.66 us (2%)
  local copies, waits for them, and re-layouts  0.62 us (2%)
    pallas_call x1, Pallas kernels, shards(): pl.pallas_call(kernel, out_shape=jax.ShapeDtypeStruct((TOK, HEADS * HD),...  39.7 us

profile of v4, /device:TPU:1, one launch (start us, length us, event | category | flops | bytes accessed | tf_op | source)
XLA Modules:
  0.0 41.0 jit_solution(17940412700703840943)
XLA Ops:
  0.7 39.7 %shard_map.73 = bf16[4,4096]{1,0:T(4,128)(2,1)S(1)} custom-call(s32[1]{0:T(128)S(6)} %copy.9.start_hbm, f32[1,128]{1,0:T(1,128)} %constant.2.clone.freq_hbm, bf16[4,4096]{1,0:T(4,128)(2,1)} %q_hbm.1, bf16[4,1024]{1,0:T(4,128)(2,1)} %k_hbm.1, bf16[4,1024]{1,0:T(4,128)(2,1)} %v_hbm.1, bf16[8,1024,128]{2,1,0:T(8,128)(2,1)} %ck_ref.1, bf16[8,1024,128]{2,1,0:T(8,128)(2,1)} %cv_ref.1), custom_call_target="tpu_custom_call" | custom-call | tf_op jit(solution)/shard_map/pallas_call | solution.py:284
  40.4 0.6 %copy.10 = bf16[4,4096]{1,0:T(4,128)(2,1)} copy(bf16[4,4096]{1,0:T(4,128)(2,1)S(1)} %shard_map.73) | data formatting | bytes 65536

commit v5 on v4

--- a/solution.py
+++ b/solution.py
@@ -27,6 +27,7 @@
 ORDER = (0, 1, 7, 2, 6, 3, 5, 4)
 PLACE = tuple(ORDER.index(i) for i in range(8))
 PIECES = 2
+BLOCKS = 4
 PART = NY // PIECES
 PAIR = 2
 
@@ -132,12 +133,17 @@
     def landed(target, got):
         pltpu.make_async_copy(target, target, got).wait()
 
-    for i in column:
-        half = sq.at[pl.ds(lax.rem(i, NC) * OWN, OWN)]
-        send(half, qall.at[:, kv], qsend.at[i], qrecv.at[kv], (head, i))
+    def spread(h):
+        for i in column:
+            half = sq.at[pl.ds(lax.rem(i, NC) * OWN + h * PAIR, PAIR)]
+            target = qall.at[pl.ds(h * PAIR, PAIR), kv]
+            send(half, target, qsend.at[h, i], qrecv.at[h, kv], (head, i))
+
+    spread(0)
     for d, i in zip(ORDER[1:], ring):
         place = PLACE[(NY - d) % NY]
         send(ybuf.at[0], ybuf.at[place], ysend.at[place], yrecv.at[place], (x * NY + i, kv))
+    spread(1)
     for i, source in enumerate((ck_ref, cv_ref)):
         send(
             source.at[pl.ds(theirs, OWN)], kvb.at[i, :, pl.ds(cached, cached)],
@@ -179,8 +185,6 @@
     for i, copy in enumerate(caches):
         copy.wait()
         landed(kvb.at[i, :, pl.ds(cached, cached)], csem.at[4 + i])
-    for i in column:
-        landed(qall.at[:, i], qrecv.at[i])
 
     def scores_of(j, keys):
         return lax.dot_general(
@@ -196,13 +200,26 @@
         return both[:, :HD], both[:, HD:]
 
     def on_cached(j, carry):
-        scores = scores_of(j, kvb[0, j, :old])
-        top = jnp.max(scores, 1, keepdims=True) * EXP_SCALE
-        probs = jnp.exp2(scores * EXP_SCALE - top).astype(jnp.bfloat16)
-        output, total = weigh(probs, kvb[1, j, :old])
+        block = old // BLOCKS
+        top = output = total = None
+        for n in range(BLOCKS):
+            keys = slice(n * block, (n + 1) * block)
+            scores = scores_of(j, kvb[0, j, keys])
+            here = jnp.broadcast_to(jnp.max(scores, 1, keepdims=True) * EXP_SCALE, (ALL, HD))
+            peak = here if n == 0 else jnp.maximum(top, here)
+            wide = jnp.concatenate([peak] * (block // HD), 1)
+            probs = jnp.exp2(scores * EXP_SCALE - wide).astype(jnp.bfloat16)
+            added, summed = weigh(probs, kvb[1, j, keys])
+            if n == 0:
+                output, total = added, summed
+            else:
+                keep = jnp.exp2(top - peak)
+                output = output * keep + added
+                total = total * keep + summed
+            top = peak
         acc[j] = output
         tot[j] = total
-        low[j] = jnp.broadcast_to(top, (ALL, HD))
+        low[j] = top
         return carry
 
     at_row = lax.broadcasted_iota(jnp.int32, (ALL, FRESH), 0)
@@ -221,8 +238,10 @@
 
     ss[...] = jnp.zeros_like(ss)
     for h in range(OWN // PAIR):
-        lax.fori_loop(h * PAIR, (h + 1) * PAIR, on_cached, 0)
         two = pl.ds(h * PAIR, PAIR)
+        for i in column:
+            landed(qall.at[two, i], qrecv.at[h, i])
+        lax.fori_loop(h * PAIR, (h + 1) * PAIR, on_cached, 0, unroll=True)
         for m in range(PIECES):
             for i in row:
                 landed(kvb.at[:, two, rows_of(i, m)], xrecv.at[h, m, i])
@@ -243,8 +262,8 @@
             ss[...] += jnp.sum(level, 1, keepdims=True)
         for i in back:
             send(so.at[i, two], ro.at[kv, two], osend.at[h, i], orecv.at[h, kv], (head, i))
-    for i in back:
-        send(ss.at[i], rs.at[kv], ssend.at[i], srecv.at[kv], (head, i))
+            if h == OWN // PAIR - 1:
+                send(ss.at[i], rs.at[kv], ssend.at[i], srecv.at[kv], (head, i))
     ro[kv] = so[kv]
     rs[kv] = ss[kv]
 
@@ -305,7 +324,7 @@
             pltpu.VMEM((NS, OWN, ROWS, HD), bf16),
             pltpu.VMEM((NS, 1, HD), f32),
             pltpu.VMEM((TOK, HEADS * HD), bf16),
-            dma((5,)), dma((6,)), dma((NS,)), dma((NS,)), dma((NY,)), dma((NY,)),
+            dma((5,)), dma((6,)), dma((2, NS)), dma((2, NS)), dma((NY,)), dma((NY,)),
             dma((2, PIECES, NG)), dma((2, PIECES, NG)), dma((2, NS)), dma((2, NS)), dma((NS,)), dma((NS,)),
         ],
         compiler_params=pltpu.CompilerParams(

time: 41.1 us -> 38.8 us (0.944)
  Pallas kernels: 39.7 us -> 37.4 us
    pallas_call x1, Pallas kernels: 39.7 us -> 37.4 us  [shards(): pl.pallas_call(kernel, out_shape=jax.ShapeDtypeStruct((TOK, HEADS * HD),...]
where the time goes in v5:
time: 38.8 us; the launch traced here: 38.6 us
  Pallas kernels  37.4 us (96%)
  between operations  0.66 us (2%)
  local copies, waits for them, and re-layouts  0.62 us (2%)
    pallas_call x1, Pallas kernels, shards(): pl.pallas_call(kernel, out_shape=jax.ShapeDtypeStruct((TOK, HEADS * HD),...  37.4 us

profile of v5, /device:TPU:1, one launch (start us, length us, event | category | flops | bytes accessed | tf_op | source)
XLA Modules:
  0.0 38.6 jit_solution(18139711009434184272)
XLA Ops:
  0.7 37.4 %shard_map.73 = bf16[4,4096]{1,0:T(4,128)(2,1)S(1)} custom-call(s32[1]{0:T(128)S(6)} %copy.9.start_hbm, f32[1,128]{1,0:T(1,128)} %constant.2.clone.freq_hbm, bf16[4,4096]{1,0:T(4,128)(2,1)} %q_hbm.1, bf16[4,1024]{1,0:T(4,128)(2,1)} %k_hbm.1, bf16[4,1024]{1,0:T(4,128)(2,1)} %v_hbm.1, bf16[8,1024,128]{2,1,0:T(8,128)(2,1)} %ck_ref.1, bf16[8,1024,128]{2,1,0:T(8,128)(2,1)} %cv_ref.1), custom_call_target="tpu_custom_call" | custom-call | tf_op jit(solution)/shard_map/pallas_call | solution.py:303
  38.0 0.6 %copy.10 = bf16[4,4096]{1,0:T(4,128)(2,1)} copy(bf16[4,4096]{1,0:T(4,128)(2,1)S(1)} %shard_map.73) | data formatting | bytes 65536

commit v6 on v5

--- a/solution.py
+++ b/solution.py
@@ -116,7 +116,7 @@
         part = k_ref[:, i * HD : (i + 1) * HD].astype(jnp.float32)
         turned = part * cosine + pltpu.roll(part, HD // 2, 1) * sine
         value = v_ref[:, i * HD : (i + 1) * HD].astype(jnp.float32)
-        ybuf[0, i] = jnp.concatenate([turned, value], 0).astype(jnp.bfloat16)
+        ybuf[0, i // OWN, i % OWN // PAIR, i % PAIR] = jnp.concatenate([turned, value], 0).astype(jnp.bfloat16)
 
     pl.semaphore_wait(barrier, len(peers))
 
@@ -139,10 +139,17 @@
             target = qall.at[pl.ds(h * PAIR, PAIR), kv]
             send(half, target, qsend.at[h, i], qrecv.at[h, kv], (head, i))
 
+    def along(h):
+        for d, i in zip(ORDER[1:], ring):
+            place = PLACE[(NY - d) % NY]
+            send(
+                ybuf.at[0, :, h], ybuf.at[place, :, h], ysend.at[h, place], yrecv.at[h, place],
+                (x * NY + i, kv),
+            )
+
+    along(0)
     spread(0)
-    for d, i in zip(ORDER[1:], ring):
-        place = PLACE[(NY - d) % NY]
-        send(ybuf.at[0], ybuf.at[place], ysend.at[place], yrecv.at[place], (x * NY + i, kv))
+    along(1)
     spread(1)
     for i, source in enumerate((ck_ref, cv_ref)):
         send(
@@ -154,33 +161,39 @@
 
     size = PART * TOK
 
-    def gather(m):
+    def gather(m, h):
         for i in range(m * PART, (m + 1) * PART):
             if i > 0:
-                landed(ybuf.at[i], yrecv.at[i])
-        for j in range(KVH):
-            four = [ybuf[m * PART + n, j].astype(jnp.float32) for n in range(PART)]
-            piece[m, 0, j] = jnp.concatenate([one[:TOK] for one in four], 0).astype(jnp.bfloat16)
-            piece[m, 1, j] = jnp.concatenate([one[TOK:] for one in four], 0).astype(jnp.bfloat16)
-
-    def rows_of(i, m):
-        return pl.ds(pl.multiple_of(old + (i * PIECES + m) * size, size), size)
-
-    def forward(h, m):
+                landed(ybuf.at[i, :, h], yrecv.at[h, i])
+        for k in range(NC * PAIR):
+            n, j = k // PAIR, k % PAIR
+            four = [ybuf[m * PART + p, n, h, j].astype(jnp.float32) for p in range(PART)]
+            j += n * OWN + h * PAIR
+            at = slice(m * size, (m + 1) * size)
+            piece[0, j, at] = jnp.concatenate([one[:TOK] for one in four], 0).astype(jnp.bfloat16)
+            piece[1, j, at] = jnp.concatenate([one[TOK:] for one in four], 0).astype(jnp.bfloat16)
+
+    def rows_of(i, m, count=1):
+        return pl.ds(pl.multiple_of(old + (i * PIECES + m) * size, size), count * size)
+
+    def forward(h, m, count):
         two = pl.ds(h * PAIR, PAIR)
+        at = pl.ds(m * size, count * size)
         for i in row:
-            half = piece.at[m, :, pl.ds(lax.rem(i, NC) * OWN + h * PAIR, PAIR)]
-            send(half, kvb.at[:, two, rows_of(g, m)], xsend.at[h, m, i], xrecv.at[h, m, g], of_row(i))
+            half = piece.at[:, pl.ds(lax.rem(i, NC) * OWN + h * PAIR, PAIR), at]
+            target = kvb.at[:, two, rows_of(g, m, count)]
+            send(half, target, xsend.at[h, m, i], xrecv.at[h, m, g], of_row(i))
         for j in range(h * PAIR, (h + 1) * PAIR):
             for n in range(2):
-                kvb[n, j, rows_of(g, m)] = piece[m, n, mine + j]
-
-    gather(0)
-    forward(0, 0)
-    gather(1)
-    forward(0, 1)
-    forward(1, 0)
-    forward(1, 1)
+                kvb[n, j, rows_of(g, m, count)] = piece[n, mine + j, m * size : (m + count) * size]
+
+    gather(0, 0)
+    forward(0, 0, 1)
+    gather(1, 0)
+    forward(0, 1, 1)
+    gather(0, 1)
+    gather(1, 1)
+    forward(1, 0, PIECES)
 
     for i, copy in enumerate(caches):
         copy.wait()
@@ -242,9 +255,9 @@
         for i in column:
             landed(qall.at[two, i], qrecv.at[h, i])
         lax.fori_loop(h * PAIR, (h + 1) * PAIR, on_cached, 0, unroll=True)
-        for m in range(PIECES):
+        for m in range(PIECES if h == 0 else 1):
             for i in row:
-                landed(kvb.at[:, two, rows_of(i, m)], xrecv.at[h, m, i])
+                landed(kvb.at[:, two, rows_of(i, m, h + 1)], xrecv.at[h, m, i])
         for j in range(h * PAIR, (h + 1) * PAIR):
             scores = jnp.where(visible, scores_of(j, kvb[0, j, old:]), -1e30)
             before = low[j]
@@ -313,8 +326,8 @@
             pltpu.VMEM((TOK, KVH * HD), bf16),
             pltpu.VMEM((KVH, ROWS, HD), bf16),
             pltpu.VMEM((OWN, NS, ROWS, HD), bf16),
-            pltpu.VMEM((NY, KVH, 2 * TOK, HD), bf16),
-            pltpu.VMEM((PIECES, 2, KVH, PART * TOK, HD), bf16),
+            pltpu.VMEM((NY, NC, OWN // PAIR, PAIR, 2 * TOK, HD), bf16),
+            pltpu.VMEM((2, KVH, PIECES * PART * TOK, HD), bf16),
             pltpu.VMEM((2, OWN, keys, HD), bf16),
             pltpu.VMEM((OWN, ALL, HD), f32),
             pltpu.VMEM((OWN, ALL, HD), f32),
@@ -324,7 +337,7 @@
             pltpu.VMEM((NS, OWN, ROWS, HD), bf16),
             pltpu.VMEM((NS, 1, HD), f32),
             pltpu.VMEM((TOK, HEADS * HD), bf16),
-            dma((5,)), dma((6,)), dma((2, NS)), dma((2, NS)), dma((NY,)), dma((NY,)),
+            dma((5,)), dma((6,)), dma((2, NS)), dma((2, NS)), dma((2, NY)), dma((2, NY)),
             dma((2, PIECES, NG)), dma((2, PIECES, NG)), dma((2, NS)), dma((2, NS)), dma((NS,)), dma((NS,)),
         ],
         compiler_params=pltpu.CompilerParams(

time: 38.8 us -> 38.7 us (level)
  no operation moved by 1% of the time
where the time goes in v6:
time: 38.7 us; the launch traced here: 38.6 us
  Pallas kernels  37.3 us (96%)
  between operations  0.66 us (2%)
  local copies, waits for them, and re-layouts  0.62 us (2%)
    pallas_call x1, Pallas kernels, shards(): pl.pallas_call(kernel, out_shape=jax.ShapeDtypeStruct((TOK, HEADS * HD),...  37.3 us

profile of v6, /device:TPU:1, one launch (start us, length us, event | category | flops | bytes accessed | tf_op | source)
XLA Modules:
  0.0 38.6 jit_solution(9372191083932906117)
XLA Ops:
  0.7 37.3 %shard_map.73 = bf16[4,4096]{1,0:T(4,128)(2,1)S(1)} custom-call(s32[1]{0:T(128)S(6)} %copy.9.start_hbm, f32[1,128]{1,0:T(1,128)} %constant.2.clone.freq_hbm, bf16[4,4096]{1,0:T(4,128)(2,1)} %q_hbm.1, bf16[4,1024]{1,0:T(4,128)(2,1)} %k_hbm.1, bf16[4,1024]{1,0:T(4,128)(2,1)} %v_hbm.1, bf16[8,1024,128]{2,1,0:T(8,128)(2,1)} %ck_ref.1, bf16[8,1024,128]{2,1,0:T(8,128)(2,1)} %cv_ref.1), custom_call_target="tpu_custom_call" | custom-call | tf_op jit(solution)/shard_map/pallas_call | solution.py:316
  38.0 0.6 %copy.10 = bf16[4,4096]{1,0:T(4,128)(2,1)} copy(bf16[4,4096]{1,0:T(4,128)(2,1)S(1)} %shard_map.73) | data formatting | bytes 65536

commit v7 on v6

--- a/solution.py
+++ b/solution.py
@@ -70,7 +70,7 @@
     peers = (
         [(head, i) for i in column] + [(x * NY + i, kv) for i in ring] + [of_row(i) for i in row]
     )
-    for device in peers:
+    for device in peers[::-1]:
         pl.semaphore_signal(barrier, inc=1, device_id=device, device_id_type=MESH)
 
     inputs = [
@@ -149,13 +149,13 @@
 
     along(0)
     spread(0)
-    along(1)
-    spread(1)
     for i, source in enumerate((ck_ref, cv_ref)):
         send(
             source.at[pl.ds(theirs, OWN)], kvb.at[i, :, pl.ds(cached, cached)],
             csem.at[2 + i], csem.at[4 + i], (head, partner),
         )
+    along(1)
+    spread(1)
     for j in range(OWN):
         qall[j, kv] = sq[mine + j]
 

time: 38.7 us -> 38.5 us (level)
  no operation moved by 1% of the time
where the time goes in v7:
time: 38.5 us; the launch traced here: 38.3 us
  Pallas kernels  37.1 us (96%)
  between operations  0.66 us (2%)
  local copies, waits for them, and re-layouts  0.62 us (2%)
    pallas_call x1, Pallas kernels, shards(): pl.pallas_call(kernel, out_shape=jax.ShapeDtypeStruct((TOK, HEADS * HD),...  37.1 us

profile of v7, /device:TPU:1, one launch (start us, length us, event | category | flops | bytes accessed | tf_op | source)
XLA Modules:
  0.0 38.3 jit_solution(7649928868361849199)
XLA Ops:
  0.7 37.1 %shard_map.73 = bf16[4,4096]{1,0:T(4,128)(2,1)S(1)} custom-call(s32[1]{0:T(128)S(6)} %copy.9.start_hbm, f32[1,128]{1,0:T(1,128)} %constant.2.clone.freq_hbm, bf16[4,4096]{1,0:T(4,128)(2,1)} %q_hbm.1, bf16[4,1024]{1,0:T(4,128)(2,1)} %k_hbm.1, bf16[4,1024]{1,0:T(4,128)(2,1)} %v_hbm.1, bf16[8,1024,128]{2,1,0:T(8,128)(2,1)} %ck_ref.1, bf16[8,1024,128]{2,1,0:T(8,128)(2,1)} %cv_ref.1), custom_call_target="tpu_custom_call" | custom-call | tf_op jit(solution)/shard_map/pallas_call | solution.py:316
  37.7 0.6 %copy.10 = bf16[4,4096]{1,0:T(4,128)(2,1)} copy(bf16[4,4096]{1,0:T(4,128)(2,1)S(1)} %shard_map.73) | data formatting | bytes 65536

commit v8 on v7

--- a/solution.py
+++ b/solution.py
@@ -27,7 +27,7 @@
 ORDER = (0, 1, 7, 2, 6, 3, 5, 4)
 PLACE = tuple(ORDER.index(i) for i in range(8))
 PIECES = 2
-BLOCKS = 4
+BLOCKS = 8
 PART = NY // PIECES
 PAIR = 2
 

time: 38.5 us -> 38.5 us (level)
  no operation moved by 1% of the time
where the time goes in v8:
time: 38.5 us; the launch traced here: 38.3 us
  Pallas kernels  37 us (96%)
  between operations  0.66 us (2%)
  local copies, waits for them, and re-layouts  0.62 us (2%)
    pallas_call x1, Pallas kernels, shards(): pl.pallas_call(kernel, out_shape=jax.ShapeDtypeStruct((TOK, HEADS * HD),...  37 us

profile of v8, /device:TPU:1, one launch (start us, length us, event | category | flops | bytes accessed | tf_op | source)
XLA Modules:
  0.0 38.3 jit_solution(7539585324098070586)
XLA Ops:
  0.7 37.0 %shard_map.73 = bf16[4,4096]{1,0:T(4,128)(2,1)S(1)} custom-call(s32[1]{0:T(128)S(6)} %copy.9.start_hbm, f32[1,128]{1,0:T(1,128)} %constant.2.clone.freq_hbm, bf16[4,4096]{1,0:T(4,128)(2,1)} %q_hbm.1, bf16[4,1024]{1,0:T(4,128)(2,1)} %k_hbm.1, bf16[4,1024]{1,0:T(4,128)(2,1)} %v_hbm.1, bf16[8,1024,128]{2,1,0:T(8,128)(2,1)} %ck_ref.1, bf16[8,1024,128]{2,1,0:T(8,128)(2,1)} %cv_ref.1), custom_call_target="tpu_custom_call" | custom-call | tf_op jit(solution)/shard_map/pallas_call | solution.py:316
  37.7 0.6 %copy.10 = bf16[4,4096]{1,0:T(4,128)(2,1)} copy(bf16[4,4096]{1,0:T(4,128)(2,1)S(1)} %shard_map.73) | data formatting | bytes 65536
